TPU v7x, 32 devices: a whole 2x2x4 slice. The times are simulated.
32 devices in a mesh: row: 8 (over z, y), col: 4 (over x, core).
Axes of the slice: x: 2, y: 2, z: 4, core: 2. Of those that a mesh axis runs over, the one named last changes fastest.
Arguments:
- queries: bfloat16 [12288, 4096], P(('row', 'col')), may hold values from -6 to 6
- keys: bfloat16 [16384, 256], P(('row', 'col')), may hold values from -6 to 6
- values: bfloat16 [16384, 256], P(('row', 'col')), may hold values from -6 to 6
- output_gradient: bfloat16 [12288, 4096], P(('row', 'col')), may hold values from -6 to 6
- tile_block_table: int32 [96, 3], P(('row', 'col')), may hold values from 0 to 31, as said below
Outputs:
- dqueries: bfloat16 [12288, 4096], P(('row', 'col'))
- dkeys: bfloat16 [16384, 256], P(('row', 'col'))
- dvalues: bfloat16 [16384, 256], P(('row', 'col'))
Inputs may be any that keep to these rules, and one draw needn't show every extreme that they name: `tile_block_table`: A tile's first id is the block that holds its own query rows; its 3 ids are distinct and none is larger than that block. Block b is held by the device of index b // 1 in the order row-major over (row, col). The tiles of one device name at most 1 distinct blocks held on devices of one col index, and at most 2 distinct blocks held on devices of one row index.
All inputs are finite; a program needn't handle non-finite values.
Results may differ from a plain program's by a relative error of at most 0.0064.
Values may be sent and summed in bfloat16 or wider, within the bound.
No kernel may reach another device: no remote copies, remote signals or barrier semaphores. Data moves between devices by JAX's collectives and lax.ppermute only.
A program may use at most 192 MiB of HBM per device.

v0:
```python
import functools
import math

import jax
import jax.numpy as jnp
from jax import lax
from jax.experimental import pallas as pl
from jax.experimental.pallas import tpu as pltpu
from jax.sharding import PartitionSpec as P

HEAD_WIDTH = 128
GROUP_WIDTH = 16
TILE_QUERY_ROWS = 128
BLOCK_KEY_ROWS = 512
PICKED_BLOCKS = 3
HEADS_STEP = 8
SCALE = HEAD_WIDTH**-0.5
SCALE_LOG2 = SCALE * math.log2(math.e)
ROWS_ROWS = (((1,), (1,)), ((), ()))
VMEM_GRANT = 67043328
AXES = ("row", "col")

F32 = jnp.float32
BF16 = jnp.bfloat16


class Layout:
    def __init__(self, mesh):
        self.n_row = mesh.shape["row"]
        self.n_col = mesh.shape["col"]
        self.ny = 1
        while self.n_row % (2 * self.ny) == 0 and 4 * self.ny * self.ny <= self.n_row:
            self.ny *= 2
        self.nz = self.n_row // self.ny
        self.plane = self.ny * self.n_col
        self.col_bits = self.n_col.bit_length() - 1
        self.y_bits = self.ny.bit_length() - 1
        assert self.n_col == 1 << self.col_bits and self.n_row == self.nz << self.y_bits

    def col_of(self, block):
        return block & (self.n_col - 1)

    def y_of(self, block):
        return (block >> self.col_bits) & (self.ny - 1)

    def ahead(self, y, c, j):
        jy, jc = divmod(j, self.n_col)
        return wrap(y + jy, self.ny) * self.n_col + wrap(c + jc, self.n_col)

    def behind(self, y, c, j):
        jy, jc = divmod(j, self.n_col)
        return wrap(y - jy, self.ny) * self.n_col + wrap(c - jc, self.n_col)

    def plane_groups(self):
        return [
            [self.device(z, y, c) for y in range(self.ny) for c in range(self.n_col)]
            for z in range(self.nz)
        ]

    def z_of(self, block):
        return block >> (self.col_bits + self.y_bits)

    def device(self, z, y, c):
        return (z * self.ny + y) * self.n_col + c

    def everyone(self):
        return [
            (z, y, c) for z in range(self.nz) for y in range(self.ny) for c in range(self.n_col)
        ]

    def along_z(self, k):
        return [
            (self.device(z, y, c), self.device((z + k) % self.nz, y, c))
            for z, y, c in self.everyone()
        ]

    def in_plane(self, j):
        jy, jc = divmod(j, self.n_col)
        return [
            (self.device(z, y, c), self.device(z, (y + jy) % self.ny, (c + jc) % self.n_col))
            for z, y, c in self.everyone()
        ]


def wrap(value, size):
    return jnp.where(value >= size, value - size, jnp.where(value < 0, value + size, value))


def hbm(count):
    return [pl.BlockSpec(memory_space=pltpu.HBM)] * count


def smem(count):
    return [pl.BlockSpec(memory_space=pltpu.SMEM)] * count


def plan_kernel(lay, place, *refs):
    tables, (send, keep) = refs[: lay.ny], refs[lay.ny :]
    z, y, c = place[0], place[1], place[2]

    def wanted(table, device_col):
        block = jnp.int32(-1)
        for entry in range(table.shape[1]):
            named = table[device_col, entry]
            block = jnp.where((lay.col_of(named) == c) & (lay.y_of(named) == y), named, block)
        return block

    for j in range(lay.plane):
        jy, jc = divmod(j, lay.n_col)
        block = wanted(tables[(lay.ny - jy) % lay.ny], wrap(c + jc, lay.n_col))
        send[j] = jnp.where(block >= 0, wrap(z - lay.z_of(block), lay.nz), 0)
        block = wanted(tables[jy], wrap(c - jc, lay.n_col))
        keep[j] = jnp.where(block >= 0, wrap(lay.z_of(block) - z, lay.nz), -1)


def make_plan(lay, place, tables):
    count = jax.ShapeDtypeStruct((lay.plane,), jnp.int32)
    return pl.pallas_call(
        lambda *refs: plan_kernel(lay, *refs),
        out_shape=[count] * 2,
        in_specs=smem(1 + lay.ny),
        out_specs=smem(2),
        compiler_params=pltpu.CompilerParams(vmem_limit_bytes=VMEM_GRANT),
        name="make_plan",
    )(place, *tables)


def select_kernel(lay, joined, place, send, *refs):
    sources = refs[-3].shape[0]
    gathered, outs = refs[:sources], refs[sources:-3]
    held, in_sems, out_sems = refs[-3:]
    y, c = place[1], place[2]
    loads = [
        pltpu.make_async_copy(gathered[k], held.at[k], in_sems.at[k]) for k in range(sources)
    ]
    for load in loads:
        load.start()
    for load in loads:
        load.wait()
    stores = []
    for j in range(lay.plane):
        target = outs[0].at[lay.ahead(y, c, j)] if joined else outs[j]
        stores.append(pltpu.make_async_copy(held.at[send[j]], target, out_sems.at[j]))
    for store in stores:
        store.start()
    for store in stores:
        store.wait()


def select_units(lay, place, send, gathered, joined):
    unit = gathered[0]
    out = jax.ShapeDtypeStruct(((lay.plane,) if joined else ()) + unit.shape, unit.dtype)
    count = 1 if joined else lay.plane
    return pl.pallas_call(
        lambda *refs: select_kernel(lay, joined, *refs),
        out_shape=[out] * count,
        in_specs=smem(2) + hbm(len(gathered)),
        out_specs=hbm(count),
        scratch_shapes=[
            pltpu.VMEM((len(gathered),) + unit.shape, unit.dtype),
            pltpu.SemaphoreType.DMA((len(gathered),)),
            pltpu.SemaphoreType.DMA((lay.plane,)),
        ],
        compiler_params=pltpu.CompilerParams(vmem_limit_bytes=VMEM_GRANT),
        name="select_units",
    )(place, send, *gathered)


def combine_kernel(lay, n_parts, place, keep, *refs):
    parts, outs = refs[:n_parts], refs[n_parts : n_parts + lay.nz]
    held, acc, sems = refs[n_parts + lay.nz :]
    y, c = place[1], place[2]
    loads = []
    for j in range(lay.plane):
        source = parts[0].at[lay.behind(y, c, j)] if n_parts == 1 else parts[j]
        loads.append(pltpu.make_async_copy(source, held.at[j], sems.at[j]))
    for j in range(lay.plane):

        @pl.when(keep[j] >= 0)
        def _(j=j):
            loads[j].start()

    acc[...] = jnp.zeros_like(acc)
    for j in range(lay.plane):

        @pl.when(keep[j] >= 0)
        def _(j=j):
            loads[j].wait()
            acc[keep[j]] += held[j].astype(F32)

    for k in range(lay.nz):
        outs[k][...] = acc[k].astype(BF16)


def combine_parts(lay, place, keep, parts):
    joined = not isinstance(parts, list)
    parts = [parts] if joined else parts
    unit = jax.ShapeDtypeStruct(parts[0].shape[-2:], parts[0].dtype)
    return pl.pallas_call(
        lambda *refs: combine_kernel(lay, len(parts), *refs),
        out_shape=[jax.ShapeDtypeStruct(unit.shape, unit.dtype)] * lay.nz,
        in_specs=smem(2) + hbm(len(parts)),
        out_specs=[pl.BlockSpec(memory_space=pltpu.VMEM)] * lay.nz,
        scratch_shapes=[
            pltpu.VMEM((lay.plane,) + unit.shape, unit.dtype),
            pltpu.VMEM((lay.nz,) + unit.shape, F32),
            pltpu.SemaphoreType.DMA((lay.plane,)),
        ],
        compiler_params=pltpu.CompilerParams(vmem_limit_bytes=VMEM_GRANT),
        name="combine_parts",
    )(place, keep, *parts)


def total_kernel(lay, widths, *refs):
    terms, (dkeys, dvalues) = refs[:-2], refs[-2:]
    for n, pieces in enumerate(widths):
        total = terms[n * lay.nz][...].astype(F32)
        for k in range(1, lay.nz):
            total += terms[n * lay.nz + k][...].astype(F32)
        total = total.astype(BF16)
        for piece, (which, g) in enumerate(pieces):
            out = (dkeys, dvalues)[which]
            out[:, g * HEAD_WIDTH : (g + 1) * HEAD_WIDTH] = total[
                :, piece * HEAD_WIDTH : (piece + 1) * HEAD_WIDTH
            ]


def total_up(lay, sums, shape):
    terms = [term for _, received in sums for term in received]
    return pl.pallas_call(
        lambda *refs: total_kernel(lay, [pieces for pieces, _ in sums], *refs),
        out_shape=[jax.ShapeDtypeStruct(shape, BF16)] * 2,
        in_specs=[pl.BlockSpec(memory_space=pltpu.VMEM)] * len(terms),
        out_specs=[pl.BlockSpec(memory_space=pltpu.VMEM)] * 2,
        compiler_params=pltpu.CompilerParams(vmem_limit_bytes=VMEM_GRANT),
        name="total_up",
    )(*terms)


def grads_kernel(lay, spec, place, lists, q, do, *refs):
    first, last, n_units, has_dq, has_carry, emit = spec
    units, refs = refs[:n_units], refs[n_units + has_dq :]
    carry, refs = (refs[0], refs[1:]) if has_carry else (None, refs)
    n_out = {"carry": 1, "joined": 1, "split": 2 * lay.n_col}[emit]
    dq, outs, refs = refs[0], refs[1 : 1 + n_out], refs[1 + n_out :]
    k_rows, v_rows, kt, acc, parts, sems, carry_sem, part_sems = refs
    y, c, tile0, start = place[1], place[2], place[3], place[4]
    t = pl.program_id(0) + first
    head = HEAD_WIDTH
    rows = HEADS_STEP * TILE_QUERY_ROWS

    @pl.when(t == first)
    def _():
        if has_carry:
            carried = pltpu.make_async_copy(carry, acc, carry_sem)
            carried.start()
        copies = []
        for column in range(lay.n_col):
            block = jnp.int32(-1)
            for tile in range(first, last):
                for pick in range(PICKED_BLOCKS):
                    named = lists[tile, pick]
                    block = jnp.where(lay.col_of(named) == column, named, block)
            from_y = lay.y_of(block)
            if n_units == 1:
                here = units[0].at[from_y * lay.n_col + column]
                pairs = [(block >= 0, [here.at[:, :head], here.at[:, head:]])]
            else:
                hops = wrap(y - from_y, lay.ny) * lay.n_col + wrap(c - column, lay.n_col)
                pairs = [
                    ((block >= 0) & (hops == j), [units[j].at[:, :head], units[j].at[:, head:]])
                    for j in range(lay.plane)
                ]
            for needed, sources in pairs:
                for n, (source, target) in enumerate(zip(sources, (k_rows, v_rows))):
                    copy = pltpu.make_async_copy(source, target.at[column], sems.at[n, column])
                    copies.append((needed, copy))
        for needed, copy in copies:
            pl.when(needed)(copy.start)
        if not has_carry:
            acc[...] = jnp.zeros_like(acc)
        for needed, copy in copies:
            pl.when(needed)(copy.wait)
        for column in range(lay.n_col):
            kt[column] = k_rows[column].T
        if has_carry:
            carried.wait()

    slots = [lay.col_of(lists[t, pick]) for pick in range(PICKED_BLOCKS)]
    offset = start + (tile0 + t) * TILE_QUERY_ROWS - lists[t, 0] * BLOCK_KEY_ROWS

    def step(own_rows, i, carry_value):
        base = pl.multiple_of(i * rows, rows)
        q_rows = jnp.concatenate([q[:, pl.ds(base + h * head, head)] for h in range(HEADS_STEP)], 0)
        do_rows = jnp.concatenate(
            [do[:, pl.ds(base + h * head, head)] for h in range(HEADS_STEP)], 0
        )
        seen = [own_rows] + [BLOCK_KEY_ROWS] * (PICKED_BLOCKS - 1)
        scores = [
            lax.dot_general(k_rows[s, :n], q_rows, ROWS_ROWS, preferred_element_type=F32)
            for s, n in zip(slots, seen)
        ]
        key_at = lax.broadcasted_iota(jnp.int32, (own_rows, rows), 0)
        query_at = lax.broadcasted_iota(jnp.int32, (own_rows, rows), 1)
        query_at = (query_at & (TILE_QUERY_ROWS - 1)) + offset
        scores[0] = jnp.where(key_at <= query_at, scores[0], -jnp.inf)
        top = jnp.max(scores[0], axis=0, keepdims=True)
        for s in scores[1:]:
            top = jnp.maximum(top, jnp.max(s, axis=0, keepdims=True))
        top = top * SCALE_LOG2
        exps = [jnp.exp2(s * SCALE_LOG2 - top) for s in scores]
        gw = [
            lax.dot_general(v_rows[s, :n], do_rows, ROWS_ROWS, preferred_element_type=F32)
            for s, n in zip(slots, seen)
        ]
        inverse = 1.0 / sum(jnp.sum(e, axis=0, keepdims=True) for e in exps)
        delta = inverse * sum(jnp.sum(e * g, axis=0, keepdims=True) for e, g in zip(exps, gw))
        dq_t = jnp.zeros((head, rows), F32)
        for s, n, e, g in zip(slots, seen, exps, gw):
            weights = e * inverse
            gs = (weights * ((g - delta) * SCALE)).astype(BF16)
            acc[s, :n, :head] += jnp.dot(gs, q_rows, preferred_element_type=F32)
            acc[s, :n, head:] += jnp.dot(
                weights.astype(BF16), do_rows, preferred_element_type=F32
            )
            dq_t += jnp.dot(kt[s, :, :n], gs, preferred_element_type=F32)
        for h in range(HEADS_STEP):
            dq[:, pl.ds(base + h * head, head)] = (
                dq_t[:, h * TILE_QUERY_ROWS : (h + 1) * TILE_QUERY_ROWS].T.astype(BF16)
            )
        return carry_value

    half = BLOCK_KEY_ROWS // 2
    for own_rows, fits in ((half, offset < half), (BLOCK_KEY_ROWS, offset >= half)):

        @pl.when(fits)
        def _(own_rows=own_rows):
            lax.fori_loop(0, GROUP_WIDTH // HEADS_STEP, functools.partial(step, own_rows), 0)

    @pl.when(t == last - 1)
    def _():
        if emit == "carry":
            copy = pltpu.make_async_copy(acc, outs[0], carry_sem)
            copy.start()
            copy.wait()
        elif emit == "joined":
            copies = []
            for column in range(lay.n_col):
                parts[column] = acc[column].astype(BF16)
                for row in range(lay.ny):
                    place_at = row * lay.n_col + column
                    copy = pltpu.make_async_copy(
                        parts.at[column], outs[0].at[place_at], part_sems.at[place_at]
                    )
                    copy.start()
                    copies.append(copy)
            for copy in copies:
                copy.wait()
        else:
            for s in range(lay.n_col):
                column = wrap(c + s, lay.n_col)
                outs[s][...] = acc[column, :, head:].astype(BF16)
                outs[lay.n_col + s][...] = acc[column, :, :head].astype(BF16)


def group_grads(lay, g, tiles, place, lists, queries, output_gradient, units, dq_in, carry, emit):
    first, last = tiles
    width = GROUP_WIDTH * HEAD_WIDTH
    wide = pl.BlockSpec((TILE_QUERY_ROWS, width), lambda t, *_: (t + first, g))
    keys_shape = (BLOCK_KEY_ROWS, HEAD_WIDTH)
    pair_shape = (BLOCK_KEY_ROWS, 2 * HEAD_WIDTH)
    acc_shape = (lay.n_col,) + pair_shape
    flat_units = list(units)
    extra = [x for x in (dq_in, carry) if x is not None]
    spec = (first, last, len(flat_units), int(dq_in is not None), carry is not None, emit)
    shapes = {
        "carry": [(acc_shape, F32)],
        "joined": [((lay.plane,) + pair_shape, BF16)],
        "split": [(keys_shape, BF16)] * (2 * lay.n_col),
    }[emit]
    flops = 10 * TILE_QUERY_ROWS * (last - first) * width * PICKED_BLOCKS * BLOCK_KEY_ROWS
    return pl.pallas_call(
        lambda *refs: grads_kernel(lay, spec, *refs),
        out_shape=[jax.ShapeDtypeStruct(queries.shape, BF16)]
        + [jax.ShapeDtypeStruct(*shape) for shape in shapes],
        grid_spec=pltpu.PrefetchScalarGridSpec(
            num_scalar_prefetch=2,
            grid=(last - first,),
            in_specs=[wide, wide] + hbm(len(flat_units) + len(extra)),
            out_specs=[wide]
            + (
                hbm(1)
                if emit != "split"
                else [pl.BlockSpec(s, lambda t, *_, n=len(s): (0,) * n) for s, _ in shapes]
            ),
            scratch_shapes=[
                pltpu.VMEM((lay.n_col,) + keys_shape, BF16),
                pltpu.VMEM((lay.n_col,) + keys_shape, BF16),
                pltpu.VMEM((lay.n_col, HEAD_WIDTH, BLOCK_KEY_ROWS), BF16),
                pltpu.VMEM(acc_shape, F32),
                pltpu.VMEM(acc_shape, BF16),
                pltpu.SemaphoreType.DMA((2, lay.plane)),
                pltpu.SemaphoreType.DMA,
                pltpu.SemaphoreType.DMA((lay.plane,)),
            ],
        ),
        input_output_aliases={} if dq_in is None else {4 + len(flat_units): 0},
        compiler_params=pltpu.CompilerParams(
            dimension_semantics=("arbitrary",), vmem_limit_bytes=VMEM_GRANT
        ),
        cost_estimate=pl.CostEstimate(
            flops=flops,
            bytes_accessed=6 * TILE_QUERY_ROWS * (last - first) * width,
            transcendentals=0,
        ),
    )(place, lists, queries, output_gradient, *flat_units, *extra)


def local(lay, queries, keys, values, output_gradient, tile_block_table):
    n_tiles = tile_block_table.shape[0]
    groups = keys.shape[1] // HEAD_WIDTH
    row, col = lax.axis_index("row"), lax.axis_index("col")
    me = row * lay.n_col + col
    devices = lay.n_row * lay.n_col
    start = devices * (keys.shape[0] - n_tiles * TILE_QUERY_ROWS)
    place = jnp.stack(
        [row >> lay.y_bits, row & (lay.ny - 1), col, me * n_tiles, jnp.int32(start)]
    ).astype(jnp.int32)

    def cut(array, g):
        return array[:, g * HEAD_WIDTH : (g + 1) * HEAD_WIDTH]

    def gather_z(unit):
        return [unit] + [lax.ppermute(unit, AXES, lay.along_z(k)) for k in range(1, lay.nz)]

    def spread(units):
        return [units[0]] + [
            lax.ppermute(units[j], AXES, lay.in_plane(j)) for j in range(1, lay.plane)
        ]

    def repeat(parts):
        return [parts[j % lay.n_col] for j in range(lay.plane)]

    def exchange(stack):
        return lax.all_to_all(
            stack, AXES, 0, 0, axis_index_groups=lay.plane_groups(), tiled=True
        )

    def finish(mine):
        return [mine[0]] + [lax.ppermute(mine[k], AXES, lay.along_z(k)) for k in range(1, lay.nz)]

    chunks = [[cut(keys, g), cut(values, g)] for g in range(groups)]
    gathered = []
    for chunk in chunks:
        gathered.append(gather_z(jnp.concatenate(chunk, axis=1)))
    flat = tile_block_table.reshape(1, n_tiles * PICKED_BLOCKS)
    table = lax.all_gather(flat, "col", axis=0, tiled=True)
    tables = [table] + [
        lax.ppermute(table, AXES, lay.in_plane(jy * lay.n_col)) for jy in range(1, lay.ny)
    ]
    send, keep = make_plan(lay, place, tables)

    landed = [spread(select_units(lay, place, send, gathered[0], False))]
    landed += [[exchange(select_units(lay, place, send, units, True)[0])] for units in gathered[1:]]
    fixed = (place, tile_block_table, queries, output_gradient)
    sums, waiting, dq = [], [], None
    for g in range(groups):
        emit = "joined" if g < groups - 1 else "split"
        dq, *parts = group_grads(
            lay, g, (0, n_tiles), *fixed, landed[g], dq, None, emit
        )
        if emit == "joined":
            waiting.append((((0, g), (1, g)), exchange(parts[0])))
    arrived, parts = lax.optimization_barrier(([units for _, units in waiting], parts))
    for (pieces, _), units in zip(waiting, arrived):
        sums.append((pieces, finish(combine_parts(lay, place, keep, units))))
    first = spread(repeat(parts[: lay.n_col]))
    second = spread(repeat(parts[lay.n_col :]))
    sums.append((((1, g),), finish(combine_parts(lay, place, keep, first))))
    sums.append((((0, g),), finish(combine_parts(lay, place, keep, second))))
    dkeys, dvalues = total_up(lay, sums, keys.shape)
    return dq, dkeys, dvalues


def solution(mesh):
    lay = Layout(mesh)
    spec = P(AXES, None)


    def body(*args):
        return local(lay, *args)

    return jax.shard_map(
        body, mesh=mesh, in_specs=(spec,) * 5, out_specs=(spec,) * 3, check_vma=False
    )
```

profile of v0, /device:TPU:27, one launch (start us, length us, event | category | flops | bytes accessed | tf_op | source)
XLA Modules:
  0.0 258.6 jit_solution(11519652193317528890)
XLA Ops:
  0.6 1.1 fusion
  1.8 0.7 pad_maximum_fusion.refs_2_
  2.5 0.2 collective-permute-start.3
  2.7 0.1 collective-permute-start.2
  2.7 3.0 %collective-permute-start.1 = (bf16[512,256]{1,0:T(8,128)(2,1)}, bf16[512,256]{1,0:T(8,128)(2,1)}, u32[]{:S(2)}, u32[]{:S(2)}) collective-permute-start(bf16[512,256]{1,0:T(8,128)(2,1)} %pad_maximum_fusion.refs_2_), channel_id=1, source_target_pairs={{0,8},{1,9},{2,10},{3,11},{4,12},{5,13},{6,14},{7,15},{8,16},{9,17... | collective-permute-start | bytes 786440 | tf_op jit(solution)/shard_map/ppermute | solution.py:434
  5.8 0.8 reshape.10
  6.5 6.1 %all-gather = s32[4,1,9]{2,1,0:T(1,128)S(1)} all-gather(s32[1,1,9]{2,1,0:T(1,128)S(1)} %reshape.10), channel_id=1, replica_groups=mesh['row'=8,'col'=4] {'col'}, dimensions={0}, use_global_device_ids=true | all-gather | bytes 180 | tf_op jit(solution)/shard_map/all_gather | solution.py:457
  12.6 1.2 collective-permute-start
  13.9 0.7 pad_maximum_fusion.1.refs_2_
  14.6 0.3 collective-permute-start.6
  14.9 0.6 collective-permute-done.refs_2_
  15.5 0.6 copy-done.1
  16.1 1.7 collective-permute-start.5
  17.8 0.0 collective-permute-done.3.refs_5_
  17.8 1.5 collective-permute-start.4
  19.3 0.6 stack.19.refs_0_
  19.9 1.7 make_plan.1
  21.6 1.1 collective-permute-done.2.refs_4_
  22.7 3.3 %select_units.2 = bf16[8,512,256]{2,1,0:T(8,128)(2,1)} custom-call(s32[5]{0:T(128)} %stack.19.refs_0_, s32[8]{0:T(128)} %get-tuple-element.47.refs_1_, bf16[512,256]{1,0:T(8,128)(2,1)} %pad_maximum_fusion.refs_2_, bf16[512,256]{1,0:T(8,128)(2,1)} %collective-permute-done.1.refs_3_, bf16[512,256]{1,0:T(8,128)(2,1)} %collective-permute-done.2.refs_4_, ...), custom_call_target="tpu_custom_call" | custom-call | tf_op jit(solution)/shard_map/select_units/pallas_call | solution.py:154
  26.0 7.5 %all-to-all-start = ((bf16[8,512,256]{2,1,0:T(8,128)(2,1)}), bf16[8,512,256]{2,1,0:T(8,128)(2,1)}, u32[]{:S(2)}, u32[]{:S(2)}) async-start(bf16[8,512,256]{2,1,0:T(8,128)(2,1)} %select_units.2), calls=%async_computation | async-start | bytes 4194304 | tf_op jit(solution)/shard_map/all_to_all | solution.py:445
  33.5 11.6 %collective-permute-done.5.refs_4_ = bf16[512,256]{1,0:T(8,128)(2,1)} collective-permute-done((bf16[512,256]{1,0:T(8,128)(2,1)}, bf16[512,256]{1,0:T(8,128)(2,1)}, u32[]{:S(2)}, u32[]{:S(2)}) %collective-permute-start.5) | collective-permute-done | bytes 262176 | tf_op jit(solution)/shard_map/ppermute | solution.py:434
  45.2 3.3 %select_units.3 = (bf16[512,256]{1,0:T(8,128)(2,1)}, bf16[512,256]{1,0:T(8,128)(2,1)}, bf16[512,256]{1,0:T(8,128)(2,1)}, bf16[512,256]{1,0:T(8,128)(2,1)}, bf16[...) custom-call(s32[5]{0:T(128)} %stack.19.refs_0_, ...), custom_call_target="tpu_custom_call" | custom-call | tf_op jit(solution)/shard_map/select_units/pallas_call | solution.py:154
  48.5 2.2 collective-permute-start.7
  50.7 1.2 collective-permute-start.8
  51.9 1.2 collective-permute-start.10
  53.1 2.0 collective-permute-start.11
  55.1 6.9 %collective-permute-done.7.refs_5_ = bf16[512,256]{1,0:T(8,128)(2,1)} collective-permute-done((bf16[512,256]{1,0:T(8,128)(2,1)}, bf16[512,256]{1,0:T(8,128)(2,1)}, u32[]{:S(2)}, u32[]{:S(2)}) %collective-permute-start.7) | collective-permute-done | bytes 262176 | tf_op jit(solution)/shard_map/ppermute | solution.py:438
  62.0 1.2 collective-permute-start.12
  63.2 5.3 %collective-permute-done.8.refs_6_ = bf16[512,256]{1,0:T(8,128)(2,1)} collective-permute-done((bf16[512,256]{1,0:T(8,128)(2,1)}, bf16[512,256]{1,0:T(8,128)(2,1)}, u32[]{:S(2)}, u32[]{:S(2)}) %collective-permute-start.8) | collective-permute-done | bytes 262176 | tf_op jit(solution)/shard_map/ppermute | solution.py:438
  68.5 0.0 collective-permute-start.13
  68.5 0.5 collective-permute-done.9.refs_7_
  68.9 4.3 %collective-permute-done.11.refs_9_ = bf16[512,256]{1,0:T(8,128)(2,1)} collective-permute-done((bf16[512,256]{1,0:T(8,128)(2,1)}, bf16[512,256]{1,0:T(8,128)(2,1)}, u32[]{:S(2)}, u32[]{:S(2)}) %collective-permute-start.11) | collective-permute-done | bytes 262176 | tf_op jit(solution)/shard_map/ppermute | solution.py:438
  73.2 7.3 %collective-permute-done.12.refs_10_ = bf16[512,256]{1,0:T(8,128)(2,1)} collective-permute-done((bf16[512,256]{1,0:T(8,128)(2,1)}, bf16[512,256]{1,0:T(8,128)(2,1)}, u32[]{:S(2)}, u32[]{:S(2)}) %collective-permute-start.12) | collective-permute-done | bytes 262176 | tf_op jit(solution)/shard_map/ppermute | solution.py:438
  80.6 1.5 collective-permute-done.13.refs_11_
  82.0 41.2 %shard_map.76 = (bf16[384,4096]{1,0:T(8,128)(2,1)}, bf16[8,512,256]{2,1,0:T(8,128)(2,1)}) custom-call(s32[5]{0:T(128)} %stack.19.refs_0_, s32[3,3]{1,0:T(4,128)} %refs_1_.3, bf16[384,4096]{1,0:T(8,128)(2,1)} %refs_2_.3, bf16[384,4096]{1,0:T(8,128)(2,1)} %refs_3_.3, bf16[512,256]{1,0:T(8,128)(2,1)} %get-tuple-element.48.refs_4_, ...), custom_call_target="tpu_custom_call" | custom-call | flops 12079595520 | bytes 4718592 | tf_op jit(solution)/shard_map/pallas_call | solution.py:382
  123.3 6.0 %all-to-all-start.1 = ((bf16[8,512,256]{2,1,0:T(8,128)(2,1)}), bf16[8,512,256]{2,1,0:T(8,128)(2,1)}, u32[]{:S(2)}, u32[]{:S(2)}) async-start(bf16[8,512,256]{2,1,0:T(8,128)(2,1)} %get-tuple-element.59), calls=%async_computation.1 | async-start | bytes 4194304 | tf_op jit(solution)/shard_map/all_to_all | solution.py:445
  129.3 40.3 %shard_map.77 = (bf16[384,4096]{1,0:T(8,128)(2,1)}, bf16[512,128]{1,0:T(8,128)(2,1)}, bf16[512,128]{1,0:T(8,128)(2,1)}, bf16[512,128]{1,0:T(8,128)(2,1)}, bf16[5...) custom-call(s32[5]{0:T(128)} %stack.19.refs_0_, ...), custom_call_target="tpu_custom_call", output_to_operand_aliasing={{0}: (5, {})} | custom-call | flops 12079595520 | bytes 4718592 | tf_op jit(solution)/shard_map/pallas_call | solution.py:382
  169.6 1.2 collective-permute-start.20
  170.8 0.0 collective-permute-start.17
  170.8 3.0 %collective-permute-start.22 = (bf16[512,128]{1,0:T(8,128)(2,1)}, bf16[512,128]{1,0:T(8,128)(2,1)}, u32[]{:S(2)}, u32[]{:S(2)}) collective-permute-start(bf16[512,128]{1,0:T(8,128)(2,1)} %get-tuple-element.75), channel_id=1, source_target_pairs={{0,6},{1,7},{2,4},{3,5},{4,2},{5,3},{6,0},{7,1},{8,14},{9,15},{10,... | collective-permute-start | bytes 393224 | tf_op jit(solution)/shard_map/ppermute | solution.py:438
  173.8 5.5 %collective-permute-start.23 = (bf16[512,128]{1,0:T(8,128)(2,1)}, bf16[512,128]{1,0:T(8,128)(2,1)}, u32[]{:S(2)}, u32[]{:S(2)}) collective-permute-start(bf16[512,128]{1,0:T(8,128)(2,1)} %get-tuple-element.76), channel_id=1, source_target_pairs={{0,7},{1,4},{2,5},{3,6},{4,3},{5,0},{6,1},{7,2},{8,15},{9,12},{10,... | collective-permute-start | bytes 393224 | tf_op jit(solution)/shard_map/ppermute | solution.py:438
  179.3 0.5 collective-permute-done.21.refs_7_
  179.8 1.1 collective-permute-start.30
  180.9 2.1 collective-permute-done.22.refs_8_
  182.9 0.1 collective-permute-start.31
  183.0 2.6 collective-permute-done.18.refs_4_
  185.6 0.3 collective-permute-start.32
  185.9 3.1 %combine_parts.3 = (bf16[512,256]{1,0:T(8,128)(2,1)}, bf16[512,256]{1,0:T(8,128)(2,1)}, bf16[512,256]{1,0:T(8,128)(2,1)}, bf16[512,256]{1,0:T(8,128)(2,1)}) custom-call(s32[5]{0:T(128)} %stack.19.refs_0_, s32[8]{0:T(128)} %get-tuple-element.58.refs_1_, bf16[8,512,256]{2,1,0:T(8,128)(2,1)} %all-to-all-done.1.refs_2_), custom_call_target="tpu_custom_call" | custom-call | tf_op jit(solution)/shard_map/combine_parts/pallas_call | solution.py:199
  188.9 1.6 collective-permute-start.28
  190.5 2.0 collective-permute-done.30.refs_6_
  192.5 5.8 %collective-permute-start.14 = (bf16[512,256]{1,0:T(8,128)(2,1)}, bf16[512,256]{1,0:T(8,128)(2,1)}, u32[]{:S(2)}, u32[]{:S(2)}) collective-permute-start(bf16[512,256]{1,0:T(8,128)(2,1)} %get-tuple-element.70), channel_id=1, source_target_pairs={{0,8},{1,9},{2,10},{3,11},{4,12},{5,13},{6,14},{7,15},{8,16},{9,17... | collective-permute-start | bytes 786440 | tf_op jit(solution)/shard_map/ppermute | solution.py:450
  198.3 11.5 %collective-permute-start.15 = (bf16[512,256]{1,0:T(8,128)(2,1)}, bf16[512,256]{1,0:T(8,128)(2,1)}, u32[]{:S(2)}, u32[]{:S(2)}) collective-permute-start(bf16[512,256]{1,0:T(8,128)(2,1)} %get-tuple-element.71), channel_id=1, source_target_pairs={{0,16},{1,17},{2,18},{3,19},{4,20},{5,21},{6,22},{7,23},{8,24},{9,... | collective-permute-start | bytes 786440 | tf_op jit(solution)/shard_map/ppermute | solution.py:450
  209.8 0.3 collective-permute-start.33
  210.1 0.1 collective-permute-start.29
  210.2 2.7 %combine_parts.4 = (bf16[512,128]{1,0:T(8,128)(2,1)}, bf16[512,128]{1,0:T(8,128)(2,1)}, bf16[512,128]{1,0:T(8,128)(2,1)}, bf16[512,128]{1,0:T(8,128)(2,1)}) custom-call(s32[5]{0:T(128)} %stack.19.refs_0_, s32[8]{0:T(128)} %get-tuple-element.58.refs_1_, bf16[512,128]{1,0:T(8,128)(2,1)} %get-tuple-element.73.refs_2_, ...), custom_call_target="tpu_custom_call" | custom-call | tf_op jit(solution)/shard_map/combine_parts/pallas_call | solution.py:199
  212.9 2.6 %collective-permute-done.33.refs_9_ = bf16[512,128]{1,0:T(8,128)(2,1)} collective-permute-done((bf16[512,128]{1,0:T(8,128)(2,1)}, bf16[512,128]{1,0:T(8,128)(2,1)}, u32[]{:S(2)}, u32[]{:S(2)}) %collective-permute-start.33) | collective-permute-done | bytes 131104 | tf_op jit(solution)/shard_map/ppermute | solution.py:438
  215.5 3.5 %collective-permute-start.24 = (bf16[512,128]{1,0:T(8,128)(2,1)}, bf16[512,128]{1,0:T(8,128)(2,1)}, u32[]{:S(2)}, u32[]{:S(2)}) collective-permute-start(bf16[512,128]{1,0:T(8,128)(2,1)} %get-tuple-element.78), channel_id=1, source_target_pairs={{0,8},{1,9},{2,10},{3,11},{4,12},{5,13},{6,14},{7,15},{8,16},{9,17... | collective-permute-start | bytes 393224 | tf_op jit(solution)/shard_map/ppermute | solution.py:450
  219.0 2.7 %combine_parts.5 = (bf16[512,128]{1,0:T(8,128)(2,1)}, bf16[512,128]{1,0:T(8,128)(2,1)}, bf16[512,128]{1,0:T(8,128)(2,1)}, bf16[512,128]{1,0:T(8,128)(2,1)}) custom-call(s32[5]{0:T(128)} %stack.19.refs_0_, s32[8]{0:T(128)} %get-tuple-element.58.refs_1_, bf16[512,128]{1,0:T(8,128)(2,1)} %get-tuple-element.81.refs_2_, ...), custom_call_target="tpu_custom_call" | custom-call | tf_op jit(solution)/shard_map/combine_parts/pallas_call | solution.py:199
  221.7 6.5 %collective-permute-start.26 = (bf16[512,128]{1,0:T(8,128)(2,1)}, bf16[512,128]{1,0:T(8,128)(2,1)}, u32[]{:S(2)}, u32[]{:S(2)}) collective-permute-start(bf16[512,128]{1,0:T(8,128)(2,1)} %get-tuple-element.80), channel_id=1, source_target_pairs={{0,24},{1,25},{2,26},{3,27},{4,28},{5,29},{6,30},{7,31},{8,0},{9,1... | collective-permute-start | bytes 393224 | tf_op jit(solution)/shard_map/ppermute | solution.py:450
  228.3 11.0 %collective-permute-done.15.refs_2_ = bf16[512,256]{1,0:T(8,128)(2,1)} collective-permute-done((bf16[512,256]{1,0:T(8,128)(2,1)}, bf16[512,256]{1,0:T(8,128)(2,1)}, u32[]{:S(2)}, u32[]{:S(2)}) %collective-permute-start.15) | collective-permute-done | bytes 262176 | tf_op jit(solution)/shard_map/ppermute | solution.py:450
  239.3 3.1 %collective-permute-start.36 = (bf16[512,128]{1,0:T(8,128)(2,1)}, bf16[512,128]{1,0:T(8,128)(2,1)}, u32[]{:S(2)}, u32[]{:S(2)}) collective-permute-start(bf16[512,128]{1,0:T(8,128)(2,1)} %get-tuple-element.88), channel_id=1, source_target_pairs={{0,24},{1,25},{2,26},{3,27},{4,28},{5,29},{6,30},{7,31},{8,0},{9,1... | collective-permute-start | bytes 393224 | tf_op jit(solution)/shard_map/ppermute | solution.py:450
  242.3 8.2 %collective-permute-done.25.refs_6_ = bf16[512,128]{1,0:T(8,128)(2,1)} collective-permute-done((bf16[512,128]{1,0:T(8,128)(2,1)}, bf16[512,128]{1,0:T(8,128)(2,1)}, u32[]{:S(2)}, u32[]{:S(2)}) %collective-permute-start.25) | collective-permute-done | bytes 131104 | tf_op jit(solution)/shard_map/ppermute | solution.py:450
  250.5 5.6 %collective-permute-done.35.refs_10_ = bf16[512,128]{1,0:T(8,128)(2,1)} collective-permute-done((bf16[512,128]{1,0:T(8,128)(2,1)}, bf16[512,128]{1,0:T(8,128)(2,1)}, u32[]{:S(2)}, u32[]{:S(2)}) %collective-permute-start.35) | collective-permute-done | bytes 131104 | tf_op jit(solution)/shard_map/ppermute | solution.py:450
  256.1 2.5 total_up.1
  (33 shorter events, 0.1 us)
Async XLA Ops:
  2.5 15.3 %collective-permute-start.3 = (bf16[512,256]{1,0:T(8,128)(2,1)}, bf16[512,256]{1,0:T(8,128)(2,1)}, u32[]{:S(2)}, u32[]{:S(2)}) collective-permute-start(bf16[512,256]{1,0:T(8,128)(2,1)} %pad_maximum_fusion.refs_2_), channel_id=1, source_target_pairs={{0,24},{1,25},{2,26},{3,27},{4,28},{5,29},{6,30},{7,31},{8,0},{9,1... | collective-permute-start | bytes 786440 | tf_op jit(solution)/shard_map/ppermute | solution.py:434
  2.7 20.0 %collective-permute-start.2 = (bf16[512,256]{1,0:T(8,128)(2,1)}, bf16[512,256]{1,0:T(8,128)(2,1)}, u32[]{:S(2)}, u32[]{:S(2)}) collective-permute-start(bf16[512,256]{1,0:T(8,128)(2,1)} %pad_maximum_fusion.refs_2_), channel_id=1, source_target_pairs={{0,16},{1,17},{2,18},{3,19},{4,20},{5,21},{6,22},{7,23},{8,24},{9,... | collective-permute-start | bytes 786440 | tf_op jit(solution)/shard_map/ppermute | solution.py:434
  2.7 20.0 %collective-permute-start.1 = (bf16[512,256]{1,0:T(8,128)(2,1)}, bf16[512,256]{1,0:T(8,128)(2,1)}, u32[]{:S(2)}, u32[]{:S(2)}) collective-permute-start(bf16[512,256]{1,0:T(8,128)(2,1)} %pad_maximum_fusion.refs_2_), channel_id=1, source_target_pairs={{0,8},{1,9},{2,10},{3,11},{4,12},{5,13},{6,14},{7,15},{8,16},{9,17... | collective-permute-start | bytes 786440 | tf_op jit(solution)/shard_map/ppermute | solution.py:434
  12.6 2.0 copy-start
  12.6 2.8 %collective-permute-start = (s32[4,9]{1,0:T(4,128)S(1)}, s32[4,9]{1,0:T(4,128)S(1)}, u32[]{:S(2)}, u32[]{:S(2)}) collective-permute-start(s32[4,9]{1,0:T(4,128)S(1)} %bitcast.5), channel_id=1, source_target_pairs={{0,4},{1,5},{2,6},{3,7},{4,0},{5,1},{6,2},{7,3},{8,12},{9,13},{10,... | collective-permute-start | bytes 440 | tf_op jit(solution)/shard_map/ppermute | solution.py:459
  14.6 18.9 %collective-permute-start.6 = (bf16[512,256]{1,0:T(8,128)(2,1)}, bf16[512,256]{1,0:T(8,128)(2,1)}, u32[]{:S(2)}, u32[]{:S(2)}) collective-permute-start(bf16[512,256]{1,0:T(8,128)(2,1)} %pad_maximum_fusion.1.refs_2_), channel_id=1, source_target_pairs={{0,24},{1,25},{2,26},{3,27},{4,28},{5,29},{6,30},{7,31},{8,0},{9,1... | collective-permute-start | bytes 786440 | tf_op jit(solution)/shard_map/ppermute | solution.py:434
  15.5 0.6 copy-start.1
  16.1 29.1 %collective-permute-start.5 = (bf16[512,256]{1,0:T(8,128)(2,1)}, bf16[512,256]{1,0:T(8,128)(2,1)}, u32[]{:S(2)}, u32[]{:S(2)}) collective-permute-start(bf16[512,256]{1,0:T(8,128)(2,1)} %pad_maximum_fusion.1.refs_2_), channel_id=1, source_target_pairs={{0,16},{1,17},{2,18},{3,19},{4,20},{5,21},{6,22},{7,23},{8,24},{9,... | collective-permute-start | bytes 786440 | tf_op jit(solution)/shard_map/ppermute | solution.py:434
  17.8 27.4 %collective-permute-start.4 = (bf16[512,256]{1,0:T(8,128)(2,1)}, bf16[512,256]{1,0:T(8,128)(2,1)}, u32[]{:S(2)}, u32[]{:S(2)}) collective-permute-start(bf16[512,256]{1,0:T(8,128)(2,1)} %pad_maximum_fusion.1.refs_2_), channel_id=1, source_target_pairs={{0,8},{1,9},{2,10},{3,11},{4,12},{5,13},{6,14},{7,15},{8,16},{9,17... | collective-permute-start | bytes 786440 | tf_op jit(solution)/shard_map/ppermute | solution.py:434
  26.0 97.2 %all-to-all-start = ((bf16[8,512,256]{2,1,0:T(8,128)(2,1)}), bf16[8,512,256]{2,1,0:T(8,128)(2,1)}, u32[]{:S(2)}, u32[]{:S(2)}) async-start(bf16[8,512,256]{2,1,0:T(8,128)(2,1)} %select_units.2), calls=%async_computation | async-start | bytes 4194304 | tf_op jit(solution)/shard_map/all_to_all | solution.py:445
  48.5 13.5 %collective-permute-start.7 = (bf16[512,256]{1,0:T(8,128)(2,1)}, bf16[512,256]{1,0:T(8,128)(2,1)}, u32[]{:S(2)}, u32[]{:S(2)}) collective-permute-start(bf16[512,256]{1,0:T(8,128)(2,1)} %get-tuple-element.49), channel_id=1, source_target_pairs={{0,1},{1,2},{2,3},{3,0},{4,5},{5,6},{6,7},{7,4},{8,9},{9,10},{10,1... | collective-permute-start | bytes 786440 | tf_op jit(solution)/shard_map/ppermute | solution.py:438
  50.7 17.8 %collective-permute-start.8 = (bf16[512,256]{1,0:T(8,128)(2,1)}, bf16[512,256]{1,0:T(8,128)(2,1)}, u32[]{:S(2)}, u32[]{:S(2)}) collective-permute-start(bf16[512,256]{1,0:T(8,128)(2,1)} %get-tuple-element.50), channel_id=1, source_target_pairs={{0,2},{1,3},{2,0},{3,1},{4,6},{5,7},{6,4},{7,5},{8,10},{9,11},{10,... | collective-permute-start | bytes 786440 | tf_op jit(solution)/shard_map/ppermute | solution.py:438
  51.9 17.0 %collective-permute-start.9 = (bf16[512,256]{1,0:T(8,128)(2,1)}, bf16[512,256]{1,0:T(8,128)(2,1)}, u32[]{:S(2)}, u32[]{:S(2)}) collective-permute-start(bf16[512,256]{1,0:T(8,128)(2,1)} %get-tuple-element.51), channel_id=1, source_target_pairs={{0,3},{1,0},{2,1},{3,2},{4,7},{5,4},{6,5},{7,6},{8,11},{9,8},{10,9... | collective-permute-start | bytes 786440 | tf_op jit(solution)/shard_map/ppermute | solution.py:438
  51.9 17.0 %collective-permute-start.10 = (bf16[512,256]{1,0:T(8,128)(2,1)}, bf16[512,256]{1,0:T(8,128)(2,1)}, u32[]{:S(2)}, u32[]{:S(2)}) collective-permute-start(bf16[512,256]{1,0:T(8,128)(2,1)} %get-tuple-element.52), channel_id=1, source_target_pairs={{0,4},{1,5},{2,6},{3,7},{4,0},{5,1},{6,2},{7,3},{8,12},{9,13},{10,... | collective-permute-start | bytes 786440 | tf_op jit(solution)/shard_map/ppermute | solution.py:438
  53.1 20.1 %collective-permute-start.11 = (bf16[512,256]{1,0:T(8,128)(2,1)}, bf16[512,256]{1,0:T(8,128)(2,1)}, u32[]{:S(2)}, u32[]{:S(2)}) collective-permute-start(bf16[512,256]{1,0:T(8,128)(2,1)} %get-tuple-element.53), channel_id=1, source_target_pairs={{0,5},{1,6},{2,7},{3,4},{4,1},{5,2},{6,3},{7,0},{8,13},{9,14},{10,... | collective-permute-start | bytes 786440 | tf_op jit(solution)/shard_map/ppermute | solution.py:438
  62.0 18.6 %collective-permute-start.12 = (bf16[512,256]{1,0:T(8,128)(2,1)}, bf16[512,256]{1,0:T(8,128)(2,1)}, u32[]{:S(2)}, u32[]{:S(2)}) collective-permute-start(bf16[512,256]{1,0:T(8,128)(2,1)} %get-tuple-element.54), channel_id=1, source_target_pairs={{0,6},{1,7},{2,4},{3,5},{4,2},{5,3},{6,0},{7,1},{8,14},{9,15},{10,... | collective-permute-start | bytes 786440 | tf_op jit(solution)/shard_map/ppermute | solution.py:438
  68.5 13.6 %collective-permute-start.13 = (bf16[512,256]{1,0:T(8,128)(2,1)}, bf16[512,256]{1,0:T(8,128)(2,1)}, u32[]{:S(2)}, u32[]{:S(2)}) collective-permute-start(bf16[512,256]{1,0:T(8,128)(2,1)} %get-tuple-element.55), channel_id=1, source_target_pairs={{0,7},{1,4},{2,5},{3,6},{4,3},{5,0},{6,1},{7,2},{8,15},{9,12},{10,... | collective-permute-start | bytes 786440 | tf_op jit(solution)/shard_map/ppermute | solution.py:438
  123.3 46.3 %all-to-all-start.1 = ((bf16[8,512,256]{2,1,0:T(8,128)(2,1)}), bf16[8,512,256]{2,1,0:T(8,128)(2,1)}, u32[]{:S(2)}, u32[]{:S(2)}) async-start(bf16[8,512,256]{2,1,0:T(8,128)(2,1)} %get-tuple-element.59), calls=%async_computation.1 | async-start | bytes 4194304 | tf_op jit(solution)/shard_map/all_to_all | solution.py:445
  169.6 4.2 %collective-permute-start.20 = (bf16[512,128]{1,0:T(8,128)(2,1)}, bf16[512,128]{1,0:T(8,128)(2,1)}, u32[]{:S(2)}, u32[]{:S(2)}) collective-permute-start(bf16[512,128]{1,0:T(8,128)(2,1)} %get-tuple-element.73.refs_2_), channel_id=1, source_target_pairs={{0,4},{1,5},{2,6},{3,7},{4,0},{5,1},{6,2},{7,3},{8,12},{9,13},{10,... | collective-permute-start | bytes 393224 | tf_op jit(solution)/shard_map/ppermute | solution.py:438
  170.8 9.0 %collective-permute-start.21 = (bf16[512,128]{1,0:T(8,128)(2,1)}, bf16[512,128]{1,0:T(8,128)(2,1)}, u32[]{:S(2)}, u32[]{:S(2)}) collective-permute-start(bf16[512,128]{1,0:T(8,128)(2,1)} %get-tuple-element.74), channel_id=1, source_target_pairs={{0,5},{1,6},{2,7},{3,4},{4,1},{5,2},{6,3},{7,0},{8,13},{9,14},{10,... | collective-permute-start | bytes 393224 | tf_op jit(solution)/shard_map/ppermute | solution.py:438
  170.8 9.0 %collective-permute-start.17 = (bf16[512,128]{1,0:T(8,128)(2,1)}, bf16[512,128]{1,0:T(8,128)(2,1)}, u32[]{:S(2)}, u32[]{:S(2)}) collective-permute-start(bf16[512,128]{1,0:T(8,128)(2,1)} %get-tuple-element.74), channel_id=1, source_target_pairs={{0,1},{1,2},{2,3},{3,0},{4,5},{5,6},{6,7},{7,4},{8,9},{9,10},{10,1... | collective-permute-start | bytes 393224 | tf_op jit(solution)/shard_map/ppermute | solution.py:438
  170.8 12.1 %collective-permute-start.22 = (bf16[512,128]{1,0:T(8,128)(2,1)}, bf16[512,128]{1,0:T(8,128)(2,1)}, u32[]{:S(2)}, u32[]{:S(2)}) collective-permute-start(bf16[512,128]{1,0:T(8,128)(2,1)} %get-tuple-element.75), channel_id=1, source_target_pairs={{0,6},{1,7},{2,4},{3,5},{4,2},{5,3},{6,0},{7,1},{8,14},{9,15},{10,... | collective-permute-start | bytes 393224 | tf_op jit(solution)/shard_map/ppermute | solution.py:438
  173.8 11.8 %collective-permute-start.18 = (bf16[512,128]{1,0:T(8,128)(2,1)}, bf16[512,128]{1,0:T(8,128)(2,1)}, u32[]{:S(2)}, u32[]{:S(2)}) collective-permute-start(bf16[512,128]{1,0:T(8,128)(2,1)} %get-tuple-element.75), channel_id=1, source_target_pairs={{0,2},{1,3},{2,0},{3,1},{4,6},{5,7},{6,4},{7,5},{8,10},{9,11},{10,... | collective-permute-start | bytes 393224 | tf_op jit(solution)/shard_map/ppermute | solution.py:438
  173.8 11.8 %collective-permute-start.23 = (bf16[512,128]{1,0:T(8,128)(2,1)}, bf16[512,128]{1,0:T(8,128)(2,1)}, u32[]{:S(2)}, u32[]{:S(2)}) collective-permute-start(bf16[512,128]{1,0:T(8,128)(2,1)} %get-tuple-element.76), channel_id=1, source_target_pairs={{0,7},{1,4},{2,5},{3,6},{4,3},{5,0},{6,1},{7,2},{8,15},{9,12},{10,... | collective-permute-start | bytes 393224 | tf_op jit(solution)/shard_map/ppermute | solution.py:438
  179.8 9.1 %collective-permute-start.19 = (bf16[512,128]{1,0:T(8,128)(2,1)}, bf16[512,128]{1,0:T(8,128)(2,1)}, u32[]{:S(2)}, u32[]{:S(2)}) collective-permute-start(bf16[512,128]{1,0:T(8,128)(2,1)} %get-tuple-element.76), channel_id=1, source_target_pairs={{0,3},{1,0},{2,1},{3,2},{4,7},{5,4},{6,5},{7,6},{8,11},{9,8},{10,9... | collective-permute-start | bytes 393224 | tf_op jit(solution)/shard_map/ppermute | solution.py:438
  179.8 12.7 %collective-permute-start.30 = (bf16[512,128]{1,0:T(8,128)(2,1)}, bf16[512,128]{1,0:T(8,128)(2,1)}, u32[]{:S(2)}, u32[]{:S(2)}) collective-permute-start(bf16[512,128]{1,0:T(8,128)(2,1)} %get-tuple-element.81.refs_2_), channel_id=1, source_target_pairs={{0,4},{1,5},{2,6},{3,7},{4,0},{5,1},{6,2},{7,3},{8,12},{9,13},{10,... | collective-permute-start | bytes 393224 | tf_op jit(solution)/shard_map/ppermute | solution.py:438
  182.9 15.4 %collective-permute-start.31 = (bf16[512,128]{1,0:T(8,128)(2,1)}, bf16[512,128]{1,0:T(8,128)(2,1)}, u32[]{:S(2)}, u32[]{:S(2)}) collective-permute-start(bf16[512,128]{1,0:T(8,128)(2,1)} %get-tuple-element.82), channel_id=1, source_target_pairs={{0,5},{1,6},{2,7},{3,4},{4,1},{5,2},{6,3},{7,0},{8,13},{9,14},{10,... | collective-permute-start | bytes 393224 | tf_op jit(solution)/shard_map/ppermute | solution.py:438
  185.6 24.2 %collective-permute-start.27 = (bf16[512,128]{1,0:T(8,128)(2,1)}, bf16[512,128]{1,0:T(8,128)(2,1)}, u32[]{:S(2)}, u32[]{:S(2)}) collective-permute-start(bf16[512,128]{1,0:T(8,128)(2,1)} %get-tuple-element.82), channel_id=1, source_target_pairs={{0,1},{1,2},{2,3},{3,0},{4,5},{5,6},{6,7},{7,4},{8,9},{9,10},{10,1... | collective-permute-start | bytes 393224 | tf_op jit(solution)/shard_map/ppermute | solution.py:438
  185.6 24.2 %collective-permute-start.32 = (bf16[512,128]{1,0:T(8,128)(2,1)}, bf16[512,128]{1,0:T(8,128)(2,1)}, u32[]{:S(2)}, u32[]{:S(2)}) collective-permute-start(bf16[512,128]{1,0:T(8,128)(2,1)} %get-tuple-element.83), channel_id=1, source_target_pairs={{0,6},{1,7},{2,4},{3,5},{4,2},{5,3},{6,0},{7,1},{8,14},{9,15},{10,... | collective-permute-start | bytes 393224 | tf_op jit(solution)/shard_map/ppermute | solution.py:438
  188.9 21.1 %collective-permute-start.28 = (bf16[512,128]{1,0:T(8,128)(2,1)}, bf16[512,128]{1,0:T(8,128)(2,1)}, u32[]{:S(2)}, u32[]{:S(2)}) collective-permute-start(bf16[512,128]{1,0:T(8,128)(2,1)} %get-tuple-element.83), channel_id=1, source_target_pairs={{0,2},{1,3},{2,0},{3,1},{4,6},{5,7},{6,4},{7,5},{8,10},{9,11},{10,... | collective-permute-start | bytes 393224 | tf_op jit(solution)/shard_map/ppermute | solution.py:438
  192.5 29.3 %collective-permute-start.14 = (bf16[512,256]{1,0:T(8,128)(2,1)}, bf16[512,256]{1,0:T(8,128)(2,1)}, u32[]{:S(2)}, u32[]{:S(2)}) collective-permute-start(bf16[512,256]{1,0:T(8,128)(2,1)} %get-tuple-element.70), channel_id=1, source_target_pairs={{0,8},{1,9},{2,10},{3,11},{4,12},{5,13},{6,14},{7,15},{8,16},{9,17... | collective-permute-start | bytes 786440 | tf_op jit(solution)/shard_map/ppermute | solution.py:450
  198.3 41.0 %collective-permute-start.15 = (bf16[512,256]{1,0:T(8,128)(2,1)}, bf16[512,256]{1,0:T(8,128)(2,1)}, u32[]{:S(2)}, u32[]{:S(2)}) collective-permute-start(bf16[512,256]{1,0:T(8,128)(2,1)} %get-tuple-element.71), channel_id=1, source_target_pairs={{0,16},{1,17},{2,18},{3,19},{4,20},{5,21},{6,22},{7,23},{8,24},{9,... | collective-permute-start | bytes 786440 | tf_op jit(solution)/shard_map/ppermute | solution.py:450
  209.8 29.5 %collective-permute-start.16 = (bf16[512,256]{1,0:T(8,128)(2,1)}, bf16[512,256]{1,0:T(8,128)(2,1)}, u32[]{:S(2)}, u32[]{:S(2)}) collective-permute-start(bf16[512,256]{1,0:T(8,128)(2,1)} %get-tuple-element.72), channel_id=1, source_target_pairs={{0,24},{1,25},{2,26},{3,27},{4,28},{5,29},{6,30},{7,31},{8,0},{9,1... | collective-permute-start | bytes 786440 | tf_op jit(solution)/shard_map/ppermute | solution.py:450
  209.8 5.7 %collective-permute-start.33 = (bf16[512,128]{1,0:T(8,128)(2,1)}, bf16[512,128]{1,0:T(8,128)(2,1)}, u32[]{:S(2)}, u32[]{:S(2)}) collective-permute-start(bf16[512,128]{1,0:T(8,128)(2,1)} %get-tuple-element.84), channel_id=1, source_target_pairs={{0,7},{1,4},{2,5},{3,6},{4,3},{5,0},{6,1},{7,2},{8,15},{9,12},{10,... | collective-permute-start | bytes 393224 | tf_op jit(solution)/shard_map/ppermute | solution.py:438
  210.1 8.9 %collective-permute-start.29 = (bf16[512,128]{1,0:T(8,128)(2,1)}, bf16[512,128]{1,0:T(8,128)(2,1)}, u32[]{:S(2)}, u32[]{:S(2)}) collective-permute-start(bf16[512,128]{1,0:T(8,128)(2,1)} %get-tuple-element.84), channel_id=1, source_target_pairs={{0,3},{1,0},{2,1},{3,2},{4,7},{5,4},{6,5},{7,6},{8,11},{9,8},{10,9... | collective-permute-start | bytes 393224 | tf_op jit(solution)/shard_map/ppermute | solution.py:438
  215.5 23.7 %collective-permute-start.24 = (bf16[512,128]{1,0:T(8,128)(2,1)}, bf16[512,128]{1,0:T(8,128)(2,1)}, u32[]{:S(2)}, u32[]{:S(2)}) collective-permute-start(bf16[512,128]{1,0:T(8,128)(2,1)} %get-tuple-element.78), channel_id=1, source_target_pairs={{0,8},{1,9},{2,10},{3,11},{4,12},{5,13},{6,14},{7,15},{8,16},{9,17... | collective-permute-start | bytes 393224 | tf_op jit(solution)/shard_map/ppermute | solution.py:450
  219.0 31.5 %collective-permute-start.25 = (bf16[512,128]{1,0:T(8,128)(2,1)}, bf16[512,128]{1,0:T(8,128)(2,1)}, u32[]{:S(2)}, u32[]{:S(2)}) collective-permute-start(bf16[512,128]{1,0:T(8,128)(2,1)} %get-tuple-element.79), channel_id=1, source_target_pairs={{0,16},{1,17},{2,18},{3,19},{4,20},{5,21},{6,22},{7,23},{8,24},{9,... | collective-permute-start | bytes 393224 | tf_op jit(solution)/shard_map/ppermute | solution.py:450
  221.7 28.8 %collective-permute-start.26 = (bf16[512,128]{1,0:T(8,128)(2,1)}, bf16[512,128]{1,0:T(8,128)(2,1)}, u32[]{:S(2)}, u32[]{:S(2)}) collective-permute-start(bf16[512,128]{1,0:T(8,128)(2,1)} %get-tuple-element.80), channel_id=1, source_target_pairs={{0,24},{1,25},{2,26},{3,27},{4,28},{5,29},{6,30},{7,31},{8,0},{9,1... | collective-permute-start | bytes 393224 | tf_op jit(solution)/shard_map/ppermute | solution.py:450
  239.2 11.3 %collective-permute-start.34 = (bf16[512,128]{1,0:T(8,128)(2,1)}, bf16[512,128]{1,0:T(8,128)(2,1)}, u32[]{:S(2)}, u32[]{:S(2)}) collective-permute-start(bf16[512,128]{1,0:T(8,128)(2,1)} %get-tuple-element.86), channel_id=1, source_target_pairs={{0,8},{1,9},{2,10},{3,11},{4,12},{5,13},{6,14},{7,15},{8,16},{9,17... | collective-permute-start | bytes 393224 | tf_op jit(solution)/shard_map/ppermute | solution.py:450
  239.2 16.9 %collective-permute-start.35 = (bf16[512,128]{1,0:T(8,128)(2,1)}, bf16[512,128]{1,0:T(8,128)(2,1)}, u32[]{:S(2)}, u32[]{:S(2)}) collective-permute-start(bf16[512,128]{1,0:T(8,128)(2,1)} %get-tuple-element.87), channel_id=1, source_target_pairs={{0,16},{1,17},{2,18},{3,19},{4,20},{5,21},{6,22},{7,23},{8,24},{9,... | collective-permute-start | bytes 393224 | tf_op jit(solution)/shard_map/ppermute | solution.py:450
  239.3 16.9 %collective-permute-start.36 = (bf16[512,128]{1,0:T(8,128)(2,1)}, bf16[512,128]{1,0:T(8,128)(2,1)}, u32[]{:S(2)}, u32[]{:S(2)}) collective-permute-start(bf16[512,128]{1,0:T(8,128)(2,1)} %get-tuple-element.88), channel_id=1, source_target_pairs={{0,24},{1,25},{2,26},{3,27},{4,28},{5,29},{6,30},{7,31},{8,0},{9,1... | collective-permute-start | bytes 393224 | tf_op jit(solution)/shard_map/ppermute | solution.py:450
where the time goes:
time: 259 us
  Pallas kernels  101 us (39%)
  waiting for transfers between devices  73.5 us (28%)
  starting transfers between devices  72.8 us (28%)
  blocking collectives  6.12 us (2%)
  local copies, waits for them, and re-layouts  3.1 us (1%)
    pallas_call x2, Pallas kernels, group_grads(): pl.pallas_call(lambda *refs: grads_kernel(lay, spec, *refs), out_shape=[j...  81.5 us
    ppermute x21, waiting for transfers between devices, spread(): lax.ppermute(units[j], AXES, lay.in_plane(j))  35.5 us
    ppermute x9, starting transfers between devices, finish(): lax.ppermute(mine[k], AXES, lay.along_z(k))  30.4 us
    ppermute x9, waiting for transfers between devices, finish(): lax.ppermute(mine[k], AXES, lay.along_z(k))  24.8 us
    ppermute x21, starting transfers between devices, spread(): lax.ppermute(units[j], AXES, lay.in_plane(j))  20.9 us
    all_to_all x2, starting transfers between devices, exchange(): lax.all_to_all(stack, AXES, 0, 0, axis_index_groups=lay.plane_groups(), t...  13.5 us
    ppermute x6, waiting for transfers between devices, gather_z(): lax.ppermute(unit, AXES, lay.along_z(k))  12.7 us
    pallas_call x3, Pallas kernels, combine_parts(): pl.pallas_call(lambda *refs: combine_kernel(lay, len(parts), *refs), out_...  8.54 us
  transfers between devices with their start and end apart: 39, of which 17 were waited for; matrix products, arithmetic and copies ran while one was open for 1% of the time, Pallas kernels for 38%

commit v1 on v0

--- a/solution.py
+++ b/solution.py
@@ -262,19 +262,21 @@
                     named = lists[tile, pick]
                     block = jnp.where(lay.col_of(named) == column, named, block)
             from_y = lay.y_of(block)
-            if n_units == 1:
-                here = units[0].at[from_y * lay.n_col + column]
-                pairs = [(block >= 0, [here.at[:, :head], here.at[:, head:]])]
-            else:
-                hops = wrap(y - from_y, lay.ny) * lay.n_col + wrap(c - column, lay.n_col)
-                pairs = [
-                    ((block >= 0) & (hops == j), [units[j].at[:, :head], units[j].at[:, head:]])
-                    for j in range(lay.plane)
-                ]
-            for needed, sources in pairs:
-                for n, (source, target) in enumerate(zip(sources, (k_rows, v_rows))):
-                    copy = pltpu.make_async_copy(source, target.at[column], sems.at[n, column])
-                    copies.append((needed, copy))
+            hops = wrap(y - from_y, lay.ny) * lay.n_col + wrap(c - column, lay.n_col)
+            pairs = []
+            for j in range(lay.plane):
+                needed = (block >= 0) & (hops == j)
+                if n_units == lay.plane:
+                    pairs.append((needed, 0, units[j].at[:, :head], k_rows))
+                    pairs.append((needed, 1, units[j].at[:, head:], v_rows))
+                else:
+                    pairs.append((needed, 0, units[j], k_rows))
+            if n_units > lay.plane:
+                here = units[lay.plane].at[from_y * lay.n_col + column]
+                pairs.append((block >= 0, 1, here, v_rows))
+            for needed, n, source, target in pairs:
+                copy = pltpu.make_async_copy(source, target.at[column], sems.at[n, column])
+                copies.append((needed, copy))
         for needed, copy in copies:
             pl.when(needed)(copy.start)
         if not has_carry:
@@ -449,7 +451,8 @@
     def finish(mine):
         return [mine[0]] + [lax.ppermute(mine[k], AXES, lay.along_z(k)) for k in range(1, lay.nz)]
 
-    chunks = [[cut(keys, g), cut(values, g)] for g in range(groups)]
+    chunks = [[cut(keys, 0)], [cut(values, 0)]]
+    chunks += [[cut(keys, g), cut(values, g)] for g in range(1, groups)]
     gathered = []
     for chunk in chunks:
         gathered.append(gather_z(jnp.concatenate(chunk, axis=1)))
@@ -460,8 +463,11 @@
     ]
     send, keep = make_plan(lay, place, tables)
 
-    landed = [spread(select_units(lay, place, send, gathered[0], False))]
-    landed += [[exchange(select_units(lay, place, send, units, True)[0])] for units in gathered[1:]]
+    landed = []
+    for n, units in enumerate(gathered):
+        chosen = select_units(lay, place, send, units, n == 1)
+        landed.append([exchange(chosen[0])] if n == 1 else spread(chosen))
+    landed = [landed[0] + landed[1]] + landed[2:]
     fixed = (place, tile_block_table, queries, output_gradient)
     sums, waiting, dq = [], [], None
     for g in range(groups):

time: 259 us -> 270 us (1.042)
  the two profiles are of different devices: /device:TPU:27 before, /device:TPU:0 now
where the time goes in v1:
time: 270 us; the launch traced here: 268 us
  Pallas kernels  99.8 us (37%)
  starting transfers between devices  84.7 us (31%)
  waiting for transfers between devices  72.4 us (27%)
  blocking collectives  5.05 us (2%)
  local copies, waits for them, and re-layouts  3.9 us (1%)
    pallas_call x2, Pallas kernels, group_grads(): pl.pallas_call(lambda *refs: grads_kernel(lay, spec, *refs), out_shape=[j...  78 us
    ppermute x28, waiting for transfers between devices, spread(): lax.ppermute(units[j], AXES, lay.in_plane(j))  42.6 us
    ppermute x28, starting transfers between devices, spread(): lax.ppermute(units[j], AXES, lay.in_plane(j))  41 us
    ppermute x9, starting transfers between devices, finish(): lax.ppermute(mine[k], AXES, lay.along_z(k))  21.8 us
    ppermute x9, waiting for transfers between devices, finish(): lax.ppermute(mine[k], AXES, lay.along_z(k))  15.8 us
    ppermute x9, waiting for transfers between devices, gather_z(): lax.ppermute(unit, AXES, lay.along_z(k))  12.5 us
    ppermute x9, starting transfers between devices, gather_z(): lax.ppermute(unit, AXES, lay.along_z(k))  11.6 us
    pallas_call x3, Pallas kernels, select_units(): pl.pallas_call(lambda *refs: select_kernel(lay, joined, *refs), out_shape...  8.91 us
  transfers between devices with their start and end apart: 49, of which 16 were waited for; matrix products, arithmetic and copies ran while one was open for 1% of the time, Pallas kernels for 35%

profile of v1, /device:TPU:0, one launch (start us, length us, event | category | flops | bytes accessed | tf_op | source)
XLA Modules:
  0.0 268.5 jit_solution(12205683254544106337)
XLA Ops:
  0.6 1.9 fusion
  2.5 5.1 %collective-permute-start.23 = (bf16[512,128]{1,0:T(8,128)(2,1)}, bf16[512,128]{1,0:T(8,128)(2,1)}, u32[]{:S(2)}, u32[]{:S(2)}) collective-permute-start(bf16[512,128]{1,0:T(8,128)(2,1)} %get-tuple-element.107.refs_2_), channel_id=1, source_target_pairs={{0,24},{1,25},{2,26},{3,27},{4,28},{5,29},{6,30},{7,31},{8,0},{9,1... | collective-permute-start | bytes 393224 | tf_op jit(solution)/shard_map/ppermute | solution.py:436
  7.6 1.0 collective-permute-start.21
  8.6 0.8 reshape.10
  9.4 5.0 %all-gather = s32[4,1,9]{2,1,0:T(1,128)S(1)} all-gather(s32[1,1,9]{2,1,0:T(1,128)S(1)} %reshape.10), channel_id=1, replica_groups=mesh['row'=8,'col'=4] {'col'}, dimensions={0}, use_global_device_ids=true | all-gather | bytes 180 | tf_op jit(solution)/shard_map/all_gather | solution.py:460
  15.0 1.5 collective-permute-start
  16.5 0.7 stack.19.refs_0_
  17.2 1.5 collective-permute-done.refs_2_
  18.7 1.7 make_plan.1
  20.4 2.8 %select_units.5 = bf16[8,512,128]{2,1,0:T(8,128)(2,1)} custom-call(s32[5]{0:T(128)} %stack.19.refs_0_, s32[8]{0:T(128)} %get-tuple-element.55.refs_1_, bf16[512,128]{1,0:T(8,128)(2,1)} %get-tuple-element.107.refs_2_, bf16[512,128]{1,0:T(8,128)(2,1)} %collective-permute-done.21.refs_3_, bf16[512,128]{1,0:T(8,128)(2,1)} %collective-permute-done.22.refs_4_, ...), custom_call_target="tpu_custom_call" | custom-call | tf_op jit(solution)/shard_map/select_units/pallas_call | solution.py:154
  23.2 4.3 %all-to-all-start = ((bf16[8,512,128]{2,1,0:T(8,128)(2,1)}), bf16[8,512,128]{2,1,0:T(8,128)(2,1)}, u32[]{:S(2)}, u32[]{:S(2)}) async-start(bf16[8,512,128]{2,1,0:T(8,128)(2,1)} %select_units.5), calls=%async_computation | async-start | bytes 2097152 | tf_op jit(solution)/shard_map/all_to_all | solution.py:447
  27.5 2.9 %collective-permute-start.13 = (bf16[512,128]{1,0:T(8,128)(2,1)}, bf16[512,128]{1,0:T(8,128)(2,1)}, u32[]{:S(2)}, u32[]{:S(2)}) collective-permute-start(bf16[512,128]{1,0:T(8,128)(2,1)} %get-tuple-element.112.refs_2_), channel_id=1, source_target_pairs={{0,24},{1,25},{2,26},{3,27},{4,28},{5,29},{6,30},{7,31},{8,0},{9,1... | collective-permute-start | bytes 393224 | tf_op jit(solution)/shard_map/ppermute | solution.py:436
  30.4 1.1 collective-permute-start.12
  31.5 3.2 %collective-permute-done.13.refs_5_ = bf16[512,128]{1,0:T(8,128)(2,1)} collective-permute-done((bf16[512,128]{1,0:T(8,128)(2,1)}, bf16[512,128]{1,0:T(8,128)(2,1)}, u32[]{:S(2)}, u32[]{:S(2)}) %collective-permute-start.13) | collective-permute-done | bytes 131104 | tf_op jit(solution)/shard_map/ppermute | solution.py:436
  34.6 9.3 %collective-permute-done.12.refs_4_ = bf16[512,128]{1,0:T(8,128)(2,1)} collective-permute-done((bf16[512,128]{1,0:T(8,128)(2,1)}, bf16[512,128]{1,0:T(8,128)(2,1)}, u32[]{:S(2)}, u32[]{:S(2)}) %collective-permute-start.12) | collective-permute-done | bytes 131104 | tf_op jit(solution)/shard_map/ppermute | solution.py:436
  43.9 2.8 %select_units.4 = (bf16[512,128]{1,0:T(8,128)(2,1)}, bf16[512,128]{1,0:T(8,128)(2,1)}, bf16[512,128]{1,0:T(8,128)(2,1)}, bf16[512,128]{1,0:T(8,128)(2,1)}, bf16[...) custom-call(s32[5]{0:T(128)} %stack.19.refs_0_, ...), custom_call_target="tpu_custom_call" | custom-call | tf_op jit(solution)/shard_map/select_units/pallas_call | solution.py:154
  46.8 1.7 collective-permute-start.15
  48.5 1.4 collective-permute-start.16
  49.9 1.5 collective-permute-start.17
  51.4 0.8 collective-permute-done.14.refs_5_
  52.2 2.6 collective-permute-start.19
  54.8 2.5 collective-permute-start.20
  57.3 1.7 pad_maximum_fusion.refs_2_
  59.1 1.3 collective-permute-start.2
  60.3 1.7 collective-permute-done.18.refs_9_
  62.3 1.5 collective-permute-done.20.refs_11_
  63.8 39.5 %shard_map.76 = (bf16[384,4096]{1,0:T(8,128)(2,1)}, bf16[8,512,256]{2,1,0:T(8,128)(2,1)}) custom-call(s32[5]{0:T(128)} %stack.19.refs_0_, s32[3,3]{1,0:T(4,128)} %refs_1_.3, bf16[384,4096]{1,0:T(8,128)(2,1)} %refs_2_.3, bf16[384,4096]{1,0:T(8,128)(2,1)} %refs_3_.3, bf16[512,128]{1,0:T(8,128)(2,1)} %get-tuple-element.64.refs_4_, ...), custom_call_target="tpu_custom_call" | custom-call | flops 12079595520 | bytes 4718592 | tf_op jit(solution)/shard_map/pallas_call | solution.py:384
  103.3 4.6 %all-to-all-start.1 = ((bf16[8,512,256]{2,1,0:T(8,128)(2,1)}), bf16[8,512,256]{2,1,0:T(8,128)(2,1)}, u32[]{:S(2)}, u32[]{:S(2)}) async-start(bf16[8,512,256]{2,1,0:T(8,128)(2,1)} %get-tuple-element.75), calls=%async_computation.1 | async-start | bytes 4194304 | tf_op jit(solution)/shard_map/all_to_all | solution.py:447
  107.9 3.3 %select_units.3 = (bf16[512,256]{1,0:T(8,128)(2,1)}, bf16[512,256]{1,0:T(8,128)(2,1)}, bf16[512,256]{1,0:T(8,128)(2,1)}, bf16[512,256]{1,0:T(8,128)(2,1)}, bf16[...) custom-call(s32[5]{0:T(128)} %stack.19.refs_0_, ...), custom_call_target="tpu_custom_call" | custom-call | tf_op jit(solution)/shard_map/select_units/pallas_call | solution.py:154
  111.2 0.8 collective-permute-start.4
  111.9 2.5 collective-permute-start.5
  114.5 1.4 collective-permute-start.6
  115.9 0.6 collective-permute-start.7
  116.5 21.4 %collective-permute-done.4.refs_5_ = bf16[512,256]{1,0:T(8,128)(2,1)} collective-permute-done((bf16[512,256]{1,0:T(8,128)(2,1)}, bf16[512,256]{1,0:T(8,128)(2,1)}, u32[]{:S(2)}, u32[]{:S(2)}) %collective-permute-start.4) | collective-permute-done | bytes 262176 | tf_op jit(solution)/shard_map/ppermute | solution.py:440
  137.9 2.3 collective-permute-start.9
  140.8 4.5 %collective-permute-start.10 = (bf16[512,256]{1,0:T(8,128)(2,1)}, bf16[512,256]{1,0:T(8,128)(2,1)}, u32[]{:S(2)}, u32[]{:S(2)}) collective-permute-start(bf16[512,256]{1,0:T(8,128)(2,1)} %get-tuple-element.63), channel_id=1, source_target_pairs={{0,7},{1,4},{2,5},{3,6},{4,3},{5,0},{6,1},{7,2},{8,15},{9,12},{10,... | collective-permute-start | bytes 786440 | tf_op jit(solution)/shard_map/ppermute | solution.py:440
  145.3 5.7 %collective-permute-done.8.refs_9_ = bf16[512,256]{1,0:T(8,128)(2,1)} collective-permute-done((bf16[512,256]{1,0:T(8,128)(2,1)}, bf16[512,256]{1,0:T(8,128)(2,1)}, u32[]{:S(2)}, u32[]{:S(2)}) %collective-permute-start.8) | collective-permute-done | bytes 262176 | tf_op jit(solution)/shard_map/ppermute | solution.py:440
  151.0 1.2 collective-permute-done.9.refs_10_
  152.2 7.7 %collective-permute-done.10.refs_11_ = bf16[512,256]{1,0:T(8,128)(2,1)} collective-permute-done((bf16[512,256]{1,0:T(8,128)(2,1)}, bf16[512,256]{1,0:T(8,128)(2,1)}, u32[]{:S(2)}, u32[]{:S(2)}) %collective-permute-start.10) | collective-permute-done | bytes 262176 | tf_op jit(solution)/shard_map/ppermute | solution.py:440
  159.9 38.6 %shard_map.77 = (bf16[384,4096]{1,0:T(8,128)(2,1)}, bf16[512,128]{1,0:T(8,128)(2,1)}, bf16[512,128]{1,0:T(8,128)(2,1)}, bf16[512,128]{1,0:T(8,128)(2,1)}, bf16[5...) custom-call(s32[5]{0:T(128)} %stack.19.refs_0_, ...), custom_call_target="tpu_custom_call", output_to_operand_aliasing={{0}: (12, {})} | custom-call | flops 12079595520 | bytes 4718592 | tf_op jit(solution)/shard_map/pallas_call | solution.py:384
  198.6 3.8 %collective-permute-start.27 = (bf16[512,128]{1,0:T(8,128)(2,1)}, bf16[512,128]{1,0:T(8,128)(2,1)}, u32[]{:S(2)}, u32[]{:S(2)}) collective-permute-start(bf16[512,128]{1,0:T(8,128)(2,1)} %get-tuple-element.90), channel_id=1, source_target_pairs={{0,1},{1,2},{2,3},{3,0},{4,5},{5,6},{6,7},{7,4},{8,9},{9,10},{10,1... | collective-permute-start | bytes 393224 | tf_op jit(solution)/shard_map/ppermute | solution.py:440
  202.4 1.9 collective-permute-start.28
  204.3 0.9 collective-permute-done.30.refs_6_
  205.3 5.5 %collective-permute-start.29 = (bf16[512,128]{1,0:T(8,128)(2,1)}, bf16[512,128]{1,0:T(8,128)(2,1)}, u32[]{:S(2)}, u32[]{:S(2)}) collective-permute-start(bf16[512,128]{1,0:T(8,128)(2,1)} %get-tuple-element.92), channel_id=1, source_target_pairs={{0,3},{1,0},{2,1},{3,2},{4,7},{5,4},{6,5},{7,6},{8,11},{9,8},{10,9... | collective-permute-start | bytes 393224 | tf_op jit(solution)/shard_map/ppermute | solution.py:440
  210.8 1.0 collective-permute-done.28.refs_4_
  211.8 2.1 collective-permute-start.37
  213.9 1.6 collective-permute-start.42
  215.4 3.1 %combine_parts.3 = (bf16[512,256]{1,0:T(8,128)(2,1)}, bf16[512,256]{1,0:T(8,128)(2,1)}, bf16[512,256]{1,0:T(8,128)(2,1)}, bf16[512,256]{1,0:T(8,128)(2,1)}) custom-call(s32[5]{0:T(128)} %stack.19.refs_0_, s32[8]{0:T(128)} %get-tuple-element.74.refs_1_, bf16[8,512,256]{2,1,0:T(8,128)(2,1)} %all-to-all-done.1.refs_2_), custom_call_target="tpu_custom_call" | custom-call | tf_op jit(solution)/shard_map/combine_parts/pallas_call | solution.py:199
  218.6 1.0 collective-permute-start.38
  219.6 2.3 collective-permute-start.25
  221.9 1.6 collective-permute-start.26
  223.5 1.3 collective-permute-start.43
  224.8 1.9 collective-permute-start.39
  226.6 2.8 %combine_parts.4 = (bf16[512,128]{1,0:T(8,128)(2,1)}, bf16[512,128]{1,0:T(8,128)(2,1)}, bf16[512,128]{1,0:T(8,128)(2,1)}, bf16[512,128]{1,0:T(8,128)(2,1)}) custom-call(s32[5]{0:T(128)} %stack.19.refs_0_, s32[8]{0:T(128)} %get-tuple-element.74.refs_1_, bf16[512,128]{1,0:T(8,128)(2,1)} %get-tuple-element.89.refs_2_, ...), custom_call_target="tpu_custom_call" | custom-call | tf_op jit(solution)/shard_map/combine_parts/pallas_call | solution.py:199
  229.9 1.7 collective-permute-start.35
  231.5 2.8 %combine_parts.5 = (bf16[512,128]{1,0:T(8,128)(2,1)}, bf16[512,128]{1,0:T(8,128)(2,1)}, bf16[512,128]{1,0:T(8,128)(2,1)}, bf16[512,128]{1,0:T(8,128)(2,1)}) custom-call(s32[5]{0:T(128)} %stack.19.refs_0_, s32[8]{0:T(128)} %get-tuple-element.74.refs_1_, bf16[512,128]{1,0:T(8,128)(2,1)} %get-tuple-element.97.refs_2_, ...), custom_call_target="tpu_custom_call" | custom-call | tf_op jit(solution)/shard_map/combine_parts/pallas_call | solution.py:199
  234.4 3.0 %collective-permute-start.36 = (bf16[512,128]{1,0:T(8,128)(2,1)}, bf16[512,128]{1,0:T(8,128)(2,1)}, u32[]{:S(2)}, u32[]{:S(2)}) collective-permute-start(bf16[512,128]{1,0:T(8,128)(2,1)} %get-tuple-element.96), channel_id=1, source_target_pairs={{0,24},{1,25},{2,26},{3,27},{4,28},{5,29},{6,30},{7,31},{8,0},{9,1... | collective-permute-start | bytes 393224 | tf_op jit(solution)/shard_map/ppermute | solution.py:452
  237.3 4.7 %collective-permute-done.25.refs_2_ = bf16[512,256]{1,0:T(8,128)(2,1)} collective-permute-done((bf16[512,256]{1,0:T(8,128)(2,1)}, bf16[512,256]{1,0:T(8,128)(2,1)}, u32[]{:S(2)}, u32[]{:S(2)}) %collective-permute-start.25) | collective-permute-done | bytes 262176 | tf_op jit(solution)/shard_map/ppermute | solution.py:452
  242.0 8.5 %collective-permute-start.44 = (bf16[512,128]{1,0:T(8,128)(2,1)}, bf16[512,128]{1,0:T(8,128)(2,1)}, u32[]{:S(2)}, u32[]{:S(2)}) collective-permute-start(bf16[512,128]{1,0:T(8,128)(2,1)} %get-tuple-element.102), channel_id=1, source_target_pairs={{0,8},{1,9},{2,10},{3,11},{4,12},{5,13},{6,14},{7,15},{8,16},{9,17... | collective-permute-start | bytes 393224 | tf_op jit(solution)/shard_map/ppermute | solution.py:452
  250.6 3.4 %collective-permute-start.45 = (bf16[512,128]{1,0:T(8,128)(2,1)}, bf16[512,128]{1,0:T(8,128)(2,1)}, u32[]{:S(2)}, u32[]{:S(2)}) collective-permute-start(bf16[512,128]{1,0:T(8,128)(2,1)} %get-tuple-element.103), channel_id=1, source_target_pairs={{0,16},{1,17},{2,18},{3,19},{4,20},{5,21},{6,22},{7,23},{8,24},{9,... | collective-permute-start | bytes 393224 | tf_op jit(solution)/shard_map/ppermute | solution.py:452
  254.0 0.9 collective-permute-start.46
  254.8 5.5 %collective-permute-done.35.refs_6_ = bf16[512,128]{1,0:T(8,128)(2,1)} collective-permute-done((bf16[512,128]{1,0:T(8,128)(2,1)}, bf16[512,128]{1,0:T(8,128)(2,1)}, u32[]{:S(2)}, u32[]{:S(2)}) %collective-permute-start.35) | collective-permute-done | bytes 131104 | tf_op jit(solution)/shard_map/ppermute | solution.py:452
  260.4 5.6 %collective-permute-done.45.refs_10_ = bf16[512,128]{1,0:T(8,128)(2,1)} collective-permute-done((bf16[512,128]{1,0:T(8,128)(2,1)}, bf16[512,128]{1,0:T(8,128)(2,1)}, u32[]{:S(2)}, u32[]{:S(2)}) %collective-permute-start.45) | collective-permute-done | bytes 131104 | tf_op jit(solution)/shard_map/ppermute | solution.py:452
  266.0 2.5 total_up.1
  (51 shorter events, 2.2 us)
Async XLA Ops:
  2.5 17.8 %collective-permute-start.23 = (bf16[512,128]{1,0:T(8,128)(2,1)}, bf16[512,128]{1,0:T(8,128)(2,1)}, u32[]{:S(2)}, u32[]{:S(2)}) collective-permute-start(bf16[512,128]{1,0:T(8,128)(2,1)} %get-tuple-element.107.refs_2_), channel_id=1, source_target_pairs={{0,24},{1,25},{2,26},{3,27},{4,28},{5,29},{6,30},{7,31},{8,0},{9,1... | collective-permute-start | bytes 393224 | tf_op jit(solution)/shard_map/ppermute | solution.py:436
  7.6 12.8 %collective-permute-start.22 = (bf16[512,128]{1,0:T(8,128)(2,1)}, bf16[512,128]{1,0:T(8,128)(2,1)}, u32[]{:S(2)}, u32[]{:S(2)}) collective-permute-start(bf16[512,128]{1,0:T(8,128)(2,1)} %get-tuple-element.107.refs_2_), channel_id=1, source_target_pairs={{0,16},{1,17},{2,18},{3,19},{4,20},{5,21},{6,22},{7,23},{8,24},{9,... | collective-permute-start | bytes 393224 | tf_op jit(solution)/shard_map/ppermute | solution.py:436
  7.6 12.8 %collective-permute-start.21 = (bf16[512,128]{1,0:T(8,128)(2,1)}, bf16[512,128]{1,0:T(8,128)(2,1)}, u32[]{:S(2)}, u32[]{:S(2)}) collective-permute-start(bf16[512,128]{1,0:T(8,128)(2,1)} %get-tuple-element.107.refs_2_), channel_id=1, source_target_pairs={{0,8},{1,9},{2,10},{3,11},{4,12},{5,13},{6,14},{7,15},{8,16},{9,17... | collective-permute-start | bytes 393224 | tf_op jit(solution)/shard_map/ppermute | solution.py:436
  14.4 0.6 copy-start
  15.0 3.7 %collective-permute-start = (s32[4,9]{1,0:T(4,128)S(1)}, s32[4,9]{1,0:T(4,128)}, u32[]{:S(2)}, u32[]{:S(2)}) collective-permute-start(s32[4,9]{1,0:T(4,128)S(1)} %bitcast.5), channel_id=1, source_target_pairs={{0,4},{1,5},{2,6},{3,7},{4,0},{5,1},{6,2},{7,3},{8,12},{9,13},{10,... | collective-permute-start | bytes 440 | tf_op jit(solution)/shard_map/ppermute | solution.py:462
  23.2 40.6 %all-to-all-start = ((bf16[8,512,128]{2,1,0:T(8,128)(2,1)}), bf16[8,512,128]{2,1,0:T(8,128)(2,1)}, u32[]{:S(2)}, u32[]{:S(2)}) async-start(bf16[8,512,128]{2,1,0:T(8,128)(2,1)} %select_units.5), calls=%async_computation | async-start | bytes 2097152 | tf_op jit(solution)/shard_map/all_to_all | solution.py:447
  27.5 7.2 %collective-permute-start.13 = (bf16[512,128]{1,0:T(8,128)(2,1)}, bf16[512,128]{1,0:T(8,128)(2,1)}, u32[]{:S(2)}, u32[]{:S(2)}) collective-permute-start(bf16[512,128]{1,0:T(8,128)(2,1)} %get-tuple-element.112.refs_2_), channel_id=1, source_target_pairs={{0,24},{1,25},{2,26},{3,27},{4,28},{5,29},{6,30},{7,31},{8,0},{9,1... | collective-permute-start | bytes 393224 | tf_op jit(solution)/shard_map/ppermute | solution.py:436
  30.4 13.6 %collective-permute-start.12 = (bf16[512,128]{1,0:T(8,128)(2,1)}, bf16[512,128]{1,0:T(8,128)(2,1)}, u32[]{:S(2)}, u32[]{:S(2)}) collective-permute-start(bf16[512,128]{1,0:T(8,128)(2,1)} %get-tuple-element.112.refs_2_), channel_id=1, source_target_pairs={{0,16},{1,17},{2,18},{3,19},{4,20},{5,21},{6,22},{7,23},{8,24},{9,... | collective-permute-start | bytes 393224 | tf_op jit(solution)/shard_map/ppermute | solution.py:436
  31.5 12.4 %collective-permute-start.11 = (bf16[512,128]{1,0:T(8,128)(2,1)}, bf16[512,128]{1,0:T(8,128)(2,1)}, u32[]{:S(2)}, u32[]{:S(2)}) collective-permute-start(bf16[512,128]{1,0:T(8,128)(2,1)} %get-tuple-element.112.refs_2_), channel_id=1, source_target_pairs={{0,8},{1,9},{2,10},{3,11},{4,12},{5,13},{6,14},{7,15},{8,16},{9,17... | collective-permute-start | bytes 393224 | tf_op jit(solution)/shard_map/ppermute | solution.py:436
  46.7 5.5 %collective-permute-start.14 = (bf16[512,128]{1,0:T(8,128)(2,1)}, bf16[512,128]{1,0:T(8,128)(2,1)}, u32[]{:S(2)}, u32[]{:S(2)}) collective-permute-start(bf16[512,128]{1,0:T(8,128)(2,1)} %get-tuple-element.65), channel_id=1, source_target_pairs={{0,1},{1,2},{2,3},{3,0},{4,5},{5,6},{6,7},{7,4},{8,9},{9,10},{10,1... | collective-permute-start | bytes 393224 | tf_op jit(solution)/shard_map/ppermute | solution.py:440
  46.8 8.0 %collective-permute-start.15 = (bf16[512,128]{1,0:T(8,128)(2,1)}, bf16[512,128]{1,0:T(8,128)(2,1)}, u32[]{:S(2)}, u32[]{:S(2)}) collective-permute-start(bf16[512,128]{1,0:T(8,128)(2,1)} %get-tuple-element.66), channel_id=1, source_target_pairs={{0,2},{1,3},{2,0},{3,1},{4,6},{5,7},{6,4},{7,5},{8,10},{9,11},{10,... | collective-permute-start | bytes 393224 | tf_op jit(solution)/shard_map/ppermute | solution.py:440
  48.5 10.5 %collective-permute-start.16 = (bf16[512,128]{1,0:T(8,128)(2,1)}, bf16[512,128]{1,0:T(8,128)(2,1)}, u32[]{:S(2)}, u32[]{:S(2)}) collective-permute-start(bf16[512,128]{1,0:T(8,128)(2,1)} %get-tuple-element.67), channel_id=1, source_target_pairs={{0,3},{1,0},{2,1},{3,2},{4,7},{5,4},{6,5},{7,6},{8,11},{9,8},{10,9... | collective-permute-start | bytes 393224 | tf_op jit(solution)/shard_map/ppermute | solution.py:440
  49.9 9.2 %collective-permute-start.17 = (bf16[512,128]{1,0:T(8,128)(2,1)}, bf16[512,128]{1,0:T(8,128)(2,1)}, u32[]{:S(2)}, u32[]{:S(2)}) collective-permute-start(bf16[512,128]{1,0:T(8,128)(2,1)} %get-tuple-element.68), channel_id=1, source_target_pairs={{0,4},{1,5},{2,6},{3,7},{4,0},{5,1},{6,2},{7,3},{8,12},{9,13},{10,... | collective-permute-start | bytes 393224 | tf_op jit(solution)/shard_map/ppermute | solution.py:440
  51.4 10.6 %collective-permute-start.18 = (bf16[512,128]{1,0:T(8,128)(2,1)}, bf16[512,128]{1,0:T(8,128)(2,1)}, u32[]{:S(2)}, u32[]{:S(2)}) collective-permute-start(bf16[512,128]{1,0:T(8,128)(2,1)} %get-tuple-element.69), channel_id=1, source_target_pairs={{0,5},{1,6},{2,7},{3,4},{4,1},{5,2},{6,3},{7,0},{8,13},{9,14},{10,... | collective-permute-start | bytes 393224 | tf_op jit(solution)/shard_map/ppermute | solution.py:440
  52.2 10.1 %collective-permute-start.19 = (bf16[512,128]{1,0:T(8,128)(2,1)}, bf16[512,128]{1,0:T(8,128)(2,1)}, u32[]{:S(2)}, u32[]{:S(2)}) collective-permute-start(bf16[512,128]{1,0:T(8,128)(2,1)} %get-tuple-element.70), channel_id=1, source_target_pairs={{0,6},{1,7},{2,4},{3,5},{4,2},{5,3},{6,0},{7,1},{8,14},{9,15},{10,... | collective-permute-start | bytes 393224 | tf_op jit(solution)/shard_map/ppermute | solution.py:440
  54.8 9.0 %collective-permute-start.20 = (bf16[512,128]{1,0:T(8,128)(2,1)}, bf16[512,128]{1,0:T(8,128)(2,1)}, u32[]{:S(2)}, u32[]{:S(2)}) collective-permute-start(bf16[512,128]{1,0:T(8,128)(2,1)} %get-tuple-element.71), channel_id=1, source_target_pairs={{0,7},{1,4},{2,5},{3,6},{4,3},{5,0},{6,1},{7,2},{8,15},{9,12},{10,... | collective-permute-start | bytes 393224 | tf_op jit(solution)/shard_map/ppermute | solution.py:440
  59.0 48.8 %collective-permute-start.3 = (bf16[512,256]{1,0:T(8,128)(2,1)}, bf16[512,256]{1,0:T(8,128)(2,1)}, u32[]{:S(2)}, u32[]{:S(2)}) collective-permute-start(bf16[512,256]{1,0:T(8,128)(2,1)} %pad_maximum_fusion.refs_2_), channel_id=1, source_target_pairs={{0,24},{1,25},{2,26},{3,27},{4,28},{5,29},{6,30},{7,31},{8,0},{9,1... | collective-permute-start | bytes 786440 | tf_op jit(solution)/shard_map/ppermute | solution.py:436
  59.1 48.8 %collective-permute-start.2 = (bf16[512,256]{1,0:T(8,128)(2,1)}, bf16[512,256]{1,0:T(8,128)(2,1)}, u32[]{:S(2)}, u32[]{:S(2)}) collective-permute-start(bf16[512,256]{1,0:T(8,128)(2,1)} %pad_maximum_fusion.refs_2_), channel_id=1, source_target_pairs={{0,16},{1,17},{2,18},{3,19},{4,20},{5,21},{6,22},{7,23},{8,24},{9,... | collective-permute-start | bytes 786440 | tf_op jit(solution)/shard_map/ppermute | solution.py:436
  62.0 45.9 %collective-permute-start.1 = (bf16[512,256]{1,0:T(8,128)(2,1)}, bf16[512,256]{1,0:T(8,128)(2,1)}, u32[]{:S(2)}, u32[]{:S(2)}) collective-permute-start(bf16[512,256]{1,0:T(8,128)(2,1)} %pad_maximum_fusion.refs_2_), channel_id=1, source_target_pairs={{0,8},{1,9},{2,10},{3,11},{4,12},{5,13},{6,14},{7,15},{8,16},{9,17... | collective-permute-start | bytes 786440 | tf_op jit(solution)/shard_map/ppermute | solution.py:436
  103.3 95.2 %all-to-all-start.1 = ((bf16[8,512,256]{2,1,0:T(8,128)(2,1)}), bf16[8,512,256]{2,1,0:T(8,128)(2,1)}, u32[]{:S(2)}, u32[]{:S(2)}) async-start(bf16[8,512,256]{2,1,0:T(8,128)(2,1)} %get-tuple-element.75), calls=%async_computation.1 | async-start | bytes 4194304 | tf_op jit(solution)/shard_map/all_to_all | solution.py:447
  111.2 26.7 %collective-permute-start.4 = (bf16[512,256]{1,0:T(8,128)(2,1)}, bf16[512,256]{1,0:T(8,128)(2,1)}, u32[]{:S(2)}, u32[]{:S(2)}) collective-permute-start(bf16[512,256]{1,0:T(8,128)(2,1)} %get-tuple-element.57), channel_id=1, source_target_pairs={{0,1},{1,2},{2,3},{3,0},{4,5},{5,6},{6,7},{7,4},{8,9},{9,10},{10,1... | collective-permute-start | bytes 786440 | tf_op jit(solution)/shard_map/ppermute | solution.py:440
  111.9 28.8 %collective-permute-start.5 = (bf16[512,256]{1,0:T(8,128)(2,1)}, bf16[512,256]{1,0:T(8,128)(2,1)}, u32[]{:S(2)}, u32[]{:S(2)}) collective-permute-start(bf16[512,256]{1,0:T(8,128)(2,1)} %get-tuple-element.58), channel_id=1, source_target_pairs={{0,2},{1,3},{2,0},{3,1},{4,6},{5,7},{6,4},{7,5},{8,10},{9,11},{10,... | collective-permute-start | bytes 786440 | tf_op jit(solution)/shard_map/ppermute | solution.py:440
  114.5 30.8 %collective-permute-start.6 = (bf16[512,256]{1,0:T(8,128)(2,1)}, bf16[512,256]{1,0:T(8,128)(2,1)}, u32[]{:S(2)}, u32[]{:S(2)}) collective-permute-start(bf16[512,256]{1,0:T(8,128)(2,1)} %get-tuple-element.59), channel_id=1, source_target_pairs={{0,3},{1,0},{2,1},{3,2},{4,7},{5,4},{6,5},{7,6},{8,11},{9,8},{10,9... | collective-permute-start | bytes 786440 | tf_op jit(solution)/shard_map/ppermute | solution.py:440
  115.9 29.4 %collective-permute-start.7 = (bf16[512,256]{1,0:T(8,128)(2,1)}, bf16[512,256]{1,0:T(8,128)(2,1)}, u32[]{:S(2)}, u32[]{:S(2)}) collective-permute-start(bf16[512,256]{1,0:T(8,128)(2,1)} %get-tuple-element.60), channel_id=1, source_target_pairs={{0,4},{1,5},{2,6},{3,7},{4,0},{5,1},{6,2},{7,3},{8,12},{9,13},{10,... | collective-permute-start | bytes 786440 | tf_op jit(solution)/shard_map/ppermute | solution.py:440
  116.5 34.5 %collective-permute-start.8 = (bf16[512,256]{1,0:T(8,128)(2,1)}, bf16[512,256]{1,0:T(8,128)(2,1)}, u32[]{:S(2)}, u32[]{:S(2)}) collective-permute-start(bf16[512,256]{1,0:T(8,128)(2,1)} %get-tuple-element.61), channel_id=1, source_target_pairs={{0,5},{1,6},{2,7},{3,4},{4,1},{5,2},{6,3},{7,0},{8,13},{9,14},{10,... | collective-permute-start | bytes 786440 | tf_op jit(solution)/shard_map/ppermute | solution.py:440
  137.9 14.3 %collective-permute-start.9 = (bf16[512,256]{1,0:T(8,128)(2,1)}, bf16[512,256]{1,0:T(8,128)(2,1)}, u32[]{:S(2)}, u32[]{:S(2)}) collective-permute-start(bf16[512,256]{1,0:T(8,128)(2,1)} %get-tuple-element.62), channel_id=1, source_target_pairs={{0,6},{1,7},{2,4},{3,5},{4,2},{5,3},{6,0},{7,1},{8,14},{9,15},{10,... | collective-permute-start | bytes 786440 | tf_op jit(solution)/shard_map/ppermute | solution.py:440
  140.8 19.1 %collective-permute-start.10 = (bf16[512,256]{1,0:T(8,128)(2,1)}, bf16[512,256]{1,0:T(8,128)(2,1)}, u32[]{:S(2)}, u32[]{:S(2)}) collective-permute-start(bf16[512,256]{1,0:T(8,128)(2,1)} %get-tuple-element.63), channel_id=1, source_target_pairs={{0,7},{1,4},{2,5},{3,6},{4,3},{5,0},{6,1},{7,2},{8,15},{9,12},{10,... | collective-permute-start | bytes 786440 | tf_op jit(solution)/shard_map/ppermute | solution.py:440
  198.5 6.8 %collective-permute-start.30 = (bf16[512,128]{1,0:T(8,128)(2,1)}, bf16[512,128]{1,0:T(8,128)(2,1)}, u32[]{:S(2)}, u32[]{:S(2)}) collective-permute-start(bf16[512,128]{1,0:T(8,128)(2,1)} %get-tuple-element.89.refs_2_), channel_id=1, source_target_pairs={{0,4},{1,5},{2,6},{3,7},{4,0},{5,1},{6,2},{7,3},{8,12},{9,13},{10,... | collective-permute-start | bytes 393224 | tf_op jit(solution)/shard_map/ppermute | solution.py:440
  198.6 6.7 %collective-permute-start.31 = (bf16[512,128]{1,0:T(8,128)(2,1)}, bf16[512,128]{1,0:T(8,128)(2,1)}, u32[]{:S(2)}, u32[]{:S(2)}) collective-permute-start(bf16[512,128]{1,0:T(8,128)(2,1)} %get-tuple-element.90), channel_id=1, source_target_pairs={{0,5},{1,6},{2,7},{3,4},{4,1},{5,2},{6,3},{7,0},{8,13},{9,14},{10,... | collective-permute-start | bytes 393224 | tf_op jit(solution)/shard_map/ppermute | solution.py:440
  198.6 12.1 %collective-permute-start.27 = (bf16[512,128]{1,0:T(8,128)(2,1)}, bf16[512,128]{1,0:T(8,128)(2,1)}, u32[]{:S(2)}, u32[]{:S(2)}) collective-permute-start(bf16[512,128]{1,0:T(8,128)(2,1)} %get-tuple-element.90), channel_id=1, source_target_pairs={{0,1},{1,2},{2,3},{3,0},{4,5},{5,6},{6,7},{7,4},{8,9},{9,10},{10,1... | collective-permute-start | bytes 393224 | tf_op jit(solution)/shard_map/ppermute | solution.py:440
  202.4 8.3 %collective-permute-start.32 = (bf16[512,128]{1,0:T(8,128)(2,1)}, bf16[512,128]{1,0:T(8,128)(2,1)}, u32[]{:S(2)}, u32[]{:S(2)}) collective-permute-start(bf16[512,128]{1,0:T(8,128)(2,1)} %get-tuple-element.91), channel_id=1, source_target_pairs={{0,6},{1,7},{2,4},{3,5},{4,2},{5,3},{6,0},{7,1},{8,14},{9,15},{10,... | collective-permute-start | bytes 393224 | tf_op jit(solution)/shard_map/ppermute | solution.py:440
  202.4 9.3 %collective-permute-start.28 = (bf16[512,128]{1,0:T(8,128)(2,1)}, bf16[512,128]{1,0:T(8,128)(2,1)}, u32[]{:S(2)}, u32[]{:S(2)}) collective-permute-start(bf16[512,128]{1,0:T(8,128)(2,1)} %get-tuple-element.91), channel_id=1, source_target_pairs={{0,2},{1,3},{2,0},{3,1},{4,6},{5,7},{6,4},{7,5},{8,10},{9,11},{10,... | collective-permute-start | bytes 393224 | tf_op jit(solution)/shard_map/ppermute | solution.py:440
  205.2 8.6 %collective-permute-start.33 = (bf16[512,128]{1,0:T(8,128)(2,1)}, bf16[512,128]{1,0:T(8,128)(2,1)}, u32[]{:S(2)}, u32[]{:S(2)}) collective-permute-start(bf16[512,128]{1,0:T(8,128)(2,1)} %get-tuple-element.92), channel_id=1, source_target_pairs={{0,7},{1,4},{2,5},{3,6},{4,3},{5,0},{6,1},{7,2},{8,15},{9,12},{10,... | collective-permute-start | bytes 393224 | tf_op jit(solution)/shard_map/ppermute | solution.py:440
  205.3 13.3 %collective-permute-start.29 = (bf16[512,128]{1,0:T(8,128)(2,1)}, bf16[512,128]{1,0:T(8,128)(2,1)}, u32[]{:S(2)}, u32[]{:S(2)}) collective-permute-start(bf16[512,128]{1,0:T(8,128)(2,1)} %get-tuple-element.92), channel_id=1, source_target_pairs={{0,3},{1,0},{2,1},{3,2},{4,7},{5,4},{6,5},{7,6},{8,11},{9,8},{10,9... | collective-permute-start | bytes 393224 | tf_op jit(solution)/shard_map/ppermute | solution.py:440
  210.7 8.8 %collective-permute-start.40 = (bf16[512,128]{1,0:T(8,128)(2,1)}, bf16[512,128]{1,0:T(8,128)(2,1)}, u32[]{:S(2)}, u32[]{:S(2)}) collective-permute-start(bf16[512,128]{1,0:T(8,128)(2,1)} %get-tuple-element.97.refs_2_), channel_id=1, source_target_pairs={{0,4},{1,5},{2,6},{3,7},{4,0},{5,1},{6,2},{7,3},{8,12},{9,13},{10,... | collective-permute-start | bytes 393224 | tf_op jit(solution)/shard_map/ppermute | solution.py:440
  210.7 8.8 %collective-permute-start.41 = (bf16[512,128]{1,0:T(8,128)(2,1)}, bf16[512,128]{1,0:T(8,128)(2,1)}, u32[]{:S(2)}, u32[]{:S(2)}) collective-permute-start(bf16[512,128]{1,0:T(8,128)(2,1)} %get-tuple-element.98), channel_id=1, source_target_pairs={{0,5},{1,6},{2,7},{3,4},{4,1},{5,2},{6,3},{7,0},{8,13},{9,14},{10,... | collective-permute-start | bytes 393224 | tf_op jit(solution)/shard_map/ppermute | solution.py:440
  211.8 10.1 %collective-permute-start.37 = (bf16[512,128]{1,0:T(8,128)(2,1)}, bf16[512,128]{1,0:T(8,128)(2,1)}, u32[]{:S(2)}, u32[]{:S(2)}) collective-permute-start(bf16[512,128]{1,0:T(8,128)(2,1)} %get-tuple-element.98), channel_id=1, source_target_pairs={{0,1},{1,2},{2,3},{3,0},{4,5},{5,6},{6,7},{7,4},{8,9},{9,10},{10,1... | collective-permute-start | bytes 393224 | tf_op jit(solution)/shard_map/ppermute | solution.py:440
  213.9 9.6 %collective-permute-start.42 = (bf16[512,128]{1,0:T(8,128)(2,1)}, bf16[512,128]{1,0:T(8,128)(2,1)}, u32[]{:S(2)}, u32[]{:S(2)}) collective-permute-start(bf16[512,128]{1,0:T(8,128)(2,1)} %get-tuple-element.99), channel_id=1, source_target_pairs={{0,6},{1,7},{2,4},{3,5},{4,2},{5,3},{6,0},{7,1},{8,14},{9,15},{10,... | collective-permute-start | bytes 393224 | tf_op jit(solution)/shard_map/ppermute | solution.py:440
  218.6 6.2 %collective-permute-start.38 = (bf16[512,128]{1,0:T(8,128)(2,1)}, bf16[512,128]{1,0:T(8,128)(2,1)}, u32[]{:S(2)}, u32[]{:S(2)}) collective-permute-start(bf16[512,128]{1,0:T(8,128)(2,1)} %get-tuple-element.99), channel_id=1, source_target_pairs={{0,2},{1,3},{2,0},{3,1},{4,6},{5,7},{6,4},{7,5},{8,10},{9,11},{10,... | collective-permute-start | bytes 393224 | tf_op jit(solution)/shard_map/ppermute | solution.py:440
  219.6 14.8 %collective-permute-start.24 = (bf16[512,256]{1,0:T(8,128)(2,1)}, bf16[512,256]{1,0:T(8,128)(2,1)}, u32[]{:S(2)}, u32[]{:S(2)}) collective-permute-start(bf16[512,256]{1,0:T(8,128)(2,1)} %get-tuple-element.86), channel_id=1, source_target_pairs={{0,8},{1,9},{2,10},{3,11},{4,12},{5,13},{6,14},{7,15},{8,16},{9,17... | collective-permute-start | bytes 786440 | tf_op jit(solution)/shard_map/ppermute | solution.py:452
  219.6 22.5 %collective-permute-start.25 = (bf16[512,256]{1,0:T(8,128)(2,1)}, bf16[512,256]{1,0:T(8,128)(2,1)}, u32[]{:S(2)}, u32[]{:S(2)}) collective-permute-start(bf16[512,256]{1,0:T(8,128)(2,1)} %get-tuple-element.87), channel_id=1, source_target_pairs={{0,16},{1,17},{2,18},{3,19},{4,20},{5,21},{6,22},{7,23},{8,24},{9,... | collective-permute-start | bytes 786440 | tf_op jit(solution)/shard_map/ppermute | solution.py:452
  221.9 28.7 %collective-permute-start.26 = (bf16[512,256]{1,0:T(8,128)(2,1)}, bf16[512,256]{1,0:T(8,128)(2,1)}, u32[]{:S(2)}, u32[]{:S(2)}) collective-permute-start(bf16[512,256]{1,0:T(8,128)(2,1)} %get-tuple-element.88), channel_id=1, source_target_pairs={{0,24},{1,25},{2,26},{3,27},{4,28},{5,29},{6,30},{7,31},{8,0},{9,1... | collective-permute-start | bytes 786440 | tf_op jit(solution)/shard_map/ppermute | solution.py:452
  223.5 6.0 %collective-permute-start.43 = (bf16[512,128]{1,0:T(8,128)(2,1)}, bf16[512,128]{1,0:T(8,128)(2,1)}, u32[]{:S(2)}, u32[]{:S(2)}) collective-permute-start(bf16[512,128]{1,0:T(8,128)(2,1)} %get-tuple-element.100), channel_id=1, source_target_pairs={{0,7},{1,4},{2,5},{3,6},{4,3},{5,0},{6,1},{7,2},{8,15},{9,12},{10,... | collective-permute-start | bytes 393224 | tf_op jit(solution)/shard_map/ppermute | solution.py:440
  224.8 5.1 %collective-permute-start.39 = (bf16[512,128]{1,0:T(8,128)(2,1)}, bf16[512,128]{1,0:T(8,128)(2,1)}, u32[]{:S(2)}, u32[]{:S(2)}) collective-permute-start(bf16[512,128]{1,0:T(8,128)(2,1)} %get-tuple-element.100), channel_id=1, source_target_pairs={{0,3},{1,0},{2,1},{3,2},{4,7},{5,4},{6,5},{7,6},{8,11},{9,8},{10,9... | collective-permute-start | bytes 393224 | tf_op jit(solution)/shard_map/ppermute | solution.py:440
  229.4 24.6 %collective-permute-start.34 = (bf16[512,128]{1,0:T(8,128)(2,1)}, bf16[512,128]{1,0:T(8,128)(2,1)}, u32[]{:S(2)}, u32[]{:S(2)}) collective-permute-start(bf16[512,128]{1,0:T(8,128)(2,1)} %get-tuple-element.94), channel_id=1, source_target_pairs={{0,8},{1,9},{2,10},{3,11},{4,12},{5,13},{6,14},{7,15},{8,16},{9,17... | collective-permute-start | bytes 393224 | tf_op jit(solution)/shard_map/ppermute | solution.py:452
  229.9 30.5 %collective-permute-start.35 = (bf16[512,128]{1,0:T(8,128)(2,1)}, bf16[512,128]{1,0:T(8,128)(2,1)}, u32[]{:S(2)}, u32[]{:S(2)}) collective-permute-start(bf16[512,128]{1,0:T(8,128)(2,1)} %get-tuple-element.95), channel_id=1, source_target_pairs={{0,16},{1,17},{2,18},{3,19},{4,20},{5,21},{6,22},{7,23},{8,24},{9,... | collective-permute-start | bytes 393224 | tf_op jit(solution)/shard_map/ppermute | solution.py:452
  234.4 26.0 %collective-permute-start.36 = (bf16[512,128]{1,0:T(8,128)(2,1)}, bf16[512,128]{1,0:T(8,128)(2,1)}, u32[]{:S(2)}, u32[]{:S(2)}) collective-permute-start(bf16[512,128]{1,0:T(8,128)(2,1)} %get-tuple-element.96), channel_id=1, source_target_pairs={{0,24},{1,25},{2,26},{3,27},{4,28},{5,29},{6,30},{7,31},{8,0},{9,1... | collective-permute-start | bytes 393224 | tf_op jit(solution)/shard_map/ppermute | solution.py:452
  242.0 18.3 %collective-permute-start.44 = (bf16[512,128]{1,0:T(8,128)(2,1)}, bf16[512,128]{1,0:T(8,128)(2,1)}, u32[]{:S(2)}, u32[]{:S(2)}) collective-permute-start(bf16[512,128]{1,0:T(8,128)(2,1)} %get-tuple-element.102), channel_id=1, source_target_pairs={{0,8},{1,9},{2,10},{3,11},{4,12},{5,13},{6,14},{7,15},{8,16},{9,17... | collective-permute-start | bytes 393224 | tf_op jit(solution)/shard_map/ppermute | solution.py:452
  250.6 15.4 %collective-permute-start.45 = (bf16[512,128]{1,0:T(8,128)(2,1)}, bf16[512,128]{1,0:T(8,128)(2,1)}, u32[]{:S(2)}, u32[]{:S(2)}) collective-permute-start(bf16[512,128]{1,0:T(8,128)(2,1)} %get-tuple-element.103), channel_id=1, source_target_pairs={{0,16},{1,17},{2,18},{3,19},{4,20},{5,21},{6,22},{7,23},{8,24},{9,... | collective-permute-start | bytes 393224 | tf_op jit(solution)/shard_map/ppermute | solution.py:452
  254.0 12.0 %collective-permute-start.46 = (bf16[512,128]{1,0:T(8,128)(2,1)}, bf16[512,128]{1,0:T(8,128)(2,1)}, u32[]{:S(2)}, u32[]{:S(2)}) collective-permute-start(bf16[512,128]{1,0:T(8,128)(2,1)} %get-tuple-element.104), channel_id=1, source_target_pairs={{0,24},{1,25},{2,26},{3,27},{4,28},{5,29},{6,30},{7,31},{8,0},{9,1... | collective-permute-start | bytes 393224 | tf_op jit(solution)/shard_map/ppermute | solution.py:452

commit v2 on v1

--- a/solution.py
+++ b/solution.py
@@ -211,13 +211,17 @@
     )(place, keep, *parts)
 
 
+def added(lay, terms):
+    total = terms[0][...].astype(F32)
+    for term in terms[1 : lay.nz]:
+        total += term[...].astype(F32)
+    return total.astype(BF16)
+
+
 def total_kernel(lay, widths, *refs):
     terms, (dkeys, dvalues) = refs[:-2], refs[-2:]
     for n, pieces in enumerate(widths):
-        total = terms[n * lay.nz][...].astype(F32)
-        for k in range(1, lay.nz):
-            total += terms[n * lay.nz + k][...].astype(F32)
-        total = total.astype(BF16)
+        total = added(lay, terms[n * lay.nz :])
         for piece, (which, g) in enumerate(pieces):
             out = (dkeys, dvalues)[which]
             out[:, g * HEAD_WIDTH : (g + 1) * HEAD_WIDTH] = total[
@@ -235,6 +239,24 @@
         compiler_params=pltpu.CompilerParams(vmem_limit_bytes=VMEM_GRANT),
         name="total_up",
     )(*terms)
+
+
+def last_kernel(lay, *refs):
+    refs[-1][...] = added(lay, refs[: lay.nz])
+
+
+def total_last(lay, terms, g, dkeys):
+    unit = pl.BlockSpec(terms[0].shape, lambda i: (0, 0))
+    return pl.pallas_call(
+        lambda *refs: last_kernel(lay, *refs),
+        out_shape=jax.ShapeDtypeStruct(dkeys.shape, dkeys.dtype),
+        grid=(1,),
+        in_specs=[unit] * lay.nz + hbm(1),
+        out_specs=pl.BlockSpec(terms[0].shape, lambda i: (0, g)),
+        input_output_aliases={lay.nz: 0},
+        compiler_params=pltpu.CompilerParams(vmem_limit_bytes=VMEM_GRANT),
+        name="total_last",
+    )(*terms, dkeys)
 
 
 def grads_kernel(lay, spec, place, lists, q, do, *refs):
@@ -484,16 +506,17 @@
     second = spread(repeat(parts[lay.n_col :]))
     sums.append((((1, g),), finish(combine_parts(lay, place, keep, first))))
     sums.append((((0, g),), finish(combine_parts(lay, place, keep, second))))
-    dkeys, dvalues = total_up(lay, sums, keys.shape)
+    dkeys, dvalues = total_up(lay, sums[:-1], keys.shape)
+    dkeys = total_last(lay, sums[-1][1], groups - 1, dkeys)
     return dq, dkeys, dvalues
 
 
 def solution(mesh):
-    lay = Layout(mesh)
     spec = P(AXES, None)
 
 
     def body(*args):
+        lay = Layout(mesh)
         return local(lay, *args)
 
     return jax.shard_map(

time: 270 us -> 269 us (level)
  waiting for transfers between devices: 72.4 us -> 64.4 us
  starting transfers between devices: 84.7 us -> 90.9 us
    ppermute x9, waiting for transfers between devices: 15.8 us -> 6.81 us  [finish(): lax.ppermute(mine[k], AXES, lay.along_z(k))]
    ppermute x9, starting transfers between devices: 21.8 us -> 27 us  [finish(): lax.ppermute(mine[k], AXES, lay.along_z(k))]
  transfers between devices with their start and end apart: 49 -> 49, of which waited for: 16 -> 17; matrix products, arithmetic and copies ran while one was open for 1% -> 1% of each run, Pallas kernels for 35% -> 36%
where the time goes in v2:
time: 269 us; the launch traced here: 268 us
  Pallas kernels  101 us (38%)
  starting transfers between devices  90.9 us (34%)
  waiting for transfers between devices  64.4 us (24%)
  blocking collectives  5.05 us (2%)
  local copies, waits for them, and re-layouts  3.9 us (1%)
    pallas_call x2, Pallas kernels, group_grads(): pl.pallas_call(lambda *refs: grads_kernel(lay, spec, *refs), out_shape=[j...  78 us
    ppermute x28, waiting for transfers between devices, spread(): lax.ppermute(units[j], AXES, lay.in_plane(j))  43.6 us
    ppermute x28, starting transfers between devices, spread(): lax.ppermute(units[j], AXES, lay.in_plane(j))  41.9 us
    ppermute x9, starting transfers between devices, finish(): lax.ppermute(mine[k], AXES, lay.along_z(k))  27 us
    ppermute x9, waiting for transfers between devices, gather_z(): lax.ppermute(unit, AXES, lay.along_z(k))  12.5 us
    ppermute x9, starting transfers between devices, gather_z(): lax.ppermute(unit, AXES, lay.along_z(k))  11.6 us
    pallas_call x3, Pallas kernels, select_units(): pl.pallas_call(lambda *refs: select_kernel(lay, joined, *refs), out_shape...  8.91 us
    all_to_all x2, starting transfers between devices, exchange(): lax.all_to_all(stack, AXES, 0, 0, axis_index_groups=lay.plane_groups(), t...  8.82 us
  transfers between devices with their start and end apart: 49, of which 17 were waited for; matrix products, arithmetic and copies ran while one was open for 1% of the time, Pallas kernels for 36%

profile of v2, /device:TPU:0, one launch (start us, length us, event | category | flops | bytes accessed | tf_op | source)
XLA Modules:
  0.0 268.1 jit_solution(11510961015955727856)
XLA Ops:
  0.6 1.9 fusion
  2.5 5.1 %collective-permute-start.23 = (bf16[512,128]{1,0:T(8,128)(2,1)}, bf16[512,128]{1,0:T(8,128)(2,1)}, u32[]{:S(2)}, u32[]{:S(2)}) collective-permute-start(bf16[512,128]{1,0:T(8,128)(2,1)} %get-tuple-element.107.refs_2_), channel_id=1, source_target_pairs={{0,24},{1,25},{2,26},{3,27},{4,28},{5,29},{6,30},{7,31},{8,0},{9,1... | collective-permute-start | bytes 393224 | tf_op jit(solution)/shard_map/ppermute | solution.py:458
  7.6 1.0 collective-permute-start.21
  8.6 0.8 reshape.10
  9.4 5.0 %all-gather = s32[4,1,9]{2,1,0:T(1,128)S(1)} all-gather(s32[1,1,9]{2,1,0:T(1,128)S(1)} %reshape.10), channel_id=1, replica_groups=mesh['row'=8,'col'=4] {'col'}, dimensions={0}, use_global_device_ids=true | all-gather | bytes 180 | tf_op jit(solution)/shard_map/all_gather | solution.py:482
  15.0 1.5 collective-permute-start
  16.5 0.7 stack.19.refs_0_
  17.2 1.5 collective-permute-done.refs_2_
  18.7 1.7 make_plan.1
  20.4 2.8 %select_units.5 = bf16[8,512,128]{2,1,0:T(8,128)(2,1)} custom-call(s32[5]{0:T(128)} %stack.19.refs_0_, s32[8]{0:T(128)} %get-tuple-element.55.refs_1_, bf16[512,128]{1,0:T(8,128)(2,1)} %get-tuple-element.107.refs_2_, bf16[512,128]{1,0:T(8,128)(2,1)} %collective-permute-done.21.refs_3_, bf16[512,128]{1,0:T(8,128)(2,1)} %collective-permute-done.22.refs_4_, ...), custom_call_target="tpu_custom_call" | custom-call | tf_op jit(solution)/shard_map/select_units/pallas_call | solution.py:154
  23.2 4.3 %all-to-all-start = ((bf16[8,512,128]{2,1,0:T(8,128)(2,1)}), bf16[8,512,128]{2,1,0:T(8,128)(2,1)}, u32[]{:S(2)}, u32[]{:S(2)}) async-start(bf16[8,512,128]{2,1,0:T(8,128)(2,1)} %select_units.5), calls=%async_computation | async-start | bytes 2097152 | tf_op jit(solution)/shard_map/all_to_all | solution.py:469
  27.5 2.9 %collective-permute-start.13 = (bf16[512,128]{1,0:T(8,128)(2,1)}, bf16[512,128]{1,0:T(8,128)(2,1)}, u32[]{:S(2)}, u32[]{:S(2)}) collective-permute-start(bf16[512,128]{1,0:T(8,128)(2,1)} %get-tuple-element.112.refs_2_), channel_id=1, source_target_pairs={{0,24},{1,25},{2,26},{3,27},{4,28},{5,29},{6,30},{7,31},{8,0},{9,1... | collective-permute-start | bytes 393224 | tf_op jit(solution)/shard_map/ppermute | solution.py:458
  30.4 1.1 collective-permute-start.12
  31.5 3.2 %collective-permute-done.13.refs_5_ = bf16[512,128]{1,0:T(8,128)(2,1)} collective-permute-done((bf16[512,128]{1,0:T(8,128)(2,1)}, bf16[512,128]{1,0:T(8,128)(2,1)}, u32[]{:S(2)}, u32[]{:S(2)}) %collective-permute-start.13) | collective-permute-done | bytes 131104 | tf_op jit(solution)/shard_map/ppermute | solution.py:458
  34.6 9.3 %collective-permute-done.12.refs_4_ = bf16[512,128]{1,0:T(8,128)(2,1)} collective-permute-done((bf16[512,128]{1,0:T(8,128)(2,1)}, bf16[512,128]{1,0:T(8,128)(2,1)}, u32[]{:S(2)}, u32[]{:S(2)}) %collective-permute-start.12) | collective-permute-done | bytes 131104 | tf_op jit(solution)/shard_map/ppermute | solution.py:458
  43.9 2.8 %select_units.4 = (bf16[512,128]{1,0:T(8,128)(2,1)}, bf16[512,128]{1,0:T(8,128)(2,1)}, bf16[512,128]{1,0:T(8,128)(2,1)}, bf16[512,128]{1,0:T(8,128)(2,1)}, bf16[...) custom-call(s32[5]{0:T(128)} %stack.19.refs_0_, ...), custom_call_target="tpu_custom_call" | custom-call | tf_op jit(solution)/shard_map/select_units/pallas_call | solution.py:154
  46.8 1.7 collective-permute-start.15
  48.5 1.4 collective-permute-start.16
  49.9 1.5 collective-permute-start.17
  51.4 0.8 collective-permute-done.14.refs_5_
  52.2 2.6 collective-permute-start.19
  54.8 2.5 collective-permute-start.20
  57.3 1.7 pad_maximum_fusion.refs_2_
  59.1 1.3 collective-permute-start.2
  60.3 1.7 collective-permute-done.18.refs_9_
  62.3 1.5 collective-permute-done.20.refs_11_
  63.8 39.5 %shard_map.76 = (bf16[384,4096]{1,0:T(8,128)(2,1)}, bf16[8,512,256]{2,1,0:T(8,128)(2,1)}) custom-call(s32[5]{0:T(128)} %stack.19.refs_0_, s32[3,3]{1,0:T(4,128)} %refs_1_.3, bf16[384,4096]{1,0:T(8,128)(2,1)} %refs_2_.3, bf16[384,4096]{1,0:T(8,128)(2,1)} %refs_3_.3, bf16[512,128]{1,0:T(8,128)(2,1)} %get-tuple-element.64.refs_4_, ...), custom_call_target="tpu_custom_call" | custom-call | flops 12079595520 | bytes 4718592 | tf_op jit(solution)/shard_map/pallas_call | solution.py:406
  103.3 4.6 %all-to-all-start.1 = ((bf16[8,512,256]{2,1,0:T(8,128)(2,1)}), bf16[8,512,256]{2,1,0:T(8,128)(2,1)}, u32[]{:S(2)}, u32[]{:S(2)}) async-start(bf16[8,512,256]{2,1,0:T(8,128)(2,1)} %get-tuple-element.75), calls=%async_computation.1 | async-start | bytes 4194304 | tf_op jit(solution)/shard_map/all_to_all | solution.py:469
  107.9 3.3 %select_units.3 = (bf16[512,256]{1,0:T(8,128)(2,1)}, bf16[512,256]{1,0:T(8,128)(2,1)}, bf16[512,256]{1,0:T(8,128)(2,1)}, bf16[512,256]{1,0:T(8,128)(2,1)}, bf16[...) custom-call(s32[5]{0:T(128)} %stack.19.refs_0_, ...), custom_call_target="tpu_custom_call" | custom-call | tf_op jit(solution)/shard_map/select_units/pallas_call | solution.py:154
  111.2 0.8 collective-permute-start.4
  111.9 2.5 collective-permute-start.5
  114.5 1.4 collective-permute-start.6
  115.9 0.6 collective-permute-start.7
  116.5 21.4 %collective-permute-done.4.refs_5_ = bf16[512,256]{1,0:T(8,128)(2,1)} collective-permute-done((bf16[512,256]{1,0:T(8,128)(2,1)}, bf16[512,256]{1,0:T(8,128)(2,1)}, u32[]{:S(2)}, u32[]{:S(2)}) %collective-permute-start.4) | collective-permute-done | bytes 262176 | tf_op jit(solution)/shard_map/ppermute | solution.py:462
  137.9 2.3 collective-permute-start.9
  140.8 4.5 %collective-permute-start.10 = (bf16[512,256]{1,0:T(8,128)(2,1)}, bf16[512,256]{1,0:T(8,128)(2,1)}, u32[]{:S(2)}, u32[]{:S(2)}) collective-permute-start(bf16[512,256]{1,0:T(8,128)(2,1)} %get-tuple-element.63), channel_id=1, source_target_pairs={{0,7},{1,4},{2,5},{3,6},{4,3},{5,0},{6,1},{7,2},{8,15},{9,12},{10,... | collective-permute-start | bytes 786440 | tf_op jit(solution)/shard_map/ppermute | solution.py:462
  145.3 5.7 %collective-permute-done.8.refs_9_ = bf16[512,256]{1,0:T(8,128)(2,1)} collective-permute-done((bf16[512,256]{1,0:T(8,128)(2,1)}, bf16[512,256]{1,0:T(8,128)(2,1)}, u32[]{:S(2)}, u32[]{:S(2)}) %collective-permute-start.8) | collective-permute-done | bytes 262176 | tf_op jit(solution)/shard_map/ppermute | solution.py:462
  151.0 1.2 collective-permute-done.9.refs_10_
  152.2 7.7 %collective-permute-done.10.refs_11_ = bf16[512,256]{1,0:T(8,128)(2,1)} collective-permute-done((bf16[512,256]{1,0:T(8,128)(2,1)}, bf16[512,256]{1,0:T(8,128)(2,1)}, u32[]{:S(2)}, u32[]{:S(2)}) %collective-permute-start.10) | collective-permute-done | bytes 262176 | tf_op jit(solution)/shard_map/ppermute | solution.py:462
  159.9 38.6 %shard_map.77 = (bf16[384,4096]{1,0:T(8,128)(2,1)}, bf16[512,128]{1,0:T(8,128)(2,1)}, bf16[512,128]{1,0:T(8,128)(2,1)}, bf16[512,128]{1,0:T(8,128)(2,1)}, bf16[5...) custom-call(s32[5]{0:T(128)} %stack.19.refs_0_, ...), custom_call_target="tpu_custom_call", output_to_operand_aliasing={{0}: (12, {})} | custom-call | flops 12079595520 | bytes 4718592 | tf_op jit(solution)/shard_map/pallas_call | solution.py:406
  198.6 3.8 %collective-permute-start.24 = (bf16[512,128]{1,0:T(8,128)(2,1)}, bf16[512,128]{1,0:T(8,128)(2,1)}, u32[]{:S(2)}, u32[]{:S(2)}) collective-permute-start(bf16[512,128]{1,0:T(8,128)(2,1)} %get-tuple-element.85), channel_id=1, source_target_pairs={{0,1},{1,2},{2,3},{3,0},{4,5},{5,6},{6,7},{7,4},{8,9},{9,10},{10,1... | collective-permute-start | bytes 393224 | tf_op jit(solution)/shard_map/ppermute | solution.py:462
  202.4 1.9 collective-permute-start.25
  204.3 0.9 collective-permute-done.27.refs_6_
  205.2 0.7 collective-permute-start.40
  206.2 6.1 %collective-permute-start.37 = (bf16[512,128]{1,0:T(8,128)(2,1)}, bf16[512,128]{1,0:T(8,128)(2,1)}, u32[]{:S(2)}, u32[]{:S(2)}) collective-permute-start(bf16[512,128]{1,0:T(8,128)(2,1)} %get-tuple-element.98), channel_id=1, source_target_pairs={{0,1},{1,2},{2,3},{3,0},{4,5},{5,6},{6,7},{7,4},{8,9},{9,10},{10,1... | collective-permute-start | bytes 393224 | tf_op jit(solution)/shard_map/ppermute | solution.py:462
  212.3 1.9 collective-permute-start.42
  214.1 1.5 collective-permute-start.43
  215.6 3.1 %combine_parts.4 = (bf16[512,256]{1,0:T(8,128)(2,1)}, bf16[512,256]{1,0:T(8,128)(2,1)}, bf16[512,256]{1,0:T(8,128)(2,1)}, bf16[512,256]{1,0:T(8,128)(2,1)}) custom-call(s32[5]{0:T(128)} %stack.19.refs_0_, s32[8]{0:T(128)} %get-tuple-element.74.refs_1_, bf16[8,512,256]{2,1,0:T(8,128)(2,1)} %all-to-all-done.1.refs_2_), custom_call_target="tpu_custom_call" | custom-call | tf_op jit(solution)/shard_map/combine_parts/pallas_call | solution.py:199
  219.3 0.6 collective-permute-done.42.refs_8_
  219.9 2.0 collective-permute-start.35
  221.9 1.5 collective-permute-start.36
  223.4 3.4 %collective-permute-start.30 = (bf16[512,128]{1,0:T(8,128)(2,1)}, bf16[512,128]{1,0:T(8,128)(2,1)}, u32[]{:S(2)}, u32[]{:S(2)}) collective-permute-start(bf16[512,128]{1,0:T(8,128)(2,1)} %get-tuple-element.87), channel_id=1, source_target_pairs={{0,7},{1,4},{2,5},{3,6},{4,3},{5,0},{6,1},{7,2},{8,15},{9,12},{10,... | collective-permute-start | bytes 393224 | tf_op jit(solution)/shard_map/ppermute | solution.py:462
  226.8 2.8 %combine_parts.5 = (bf16[512,128]{1,0:T(8,128)(2,1)}, bf16[512,128]{1,0:T(8,128)(2,1)}, bf16[512,128]{1,0:T(8,128)(2,1)}, bf16[512,128]{1,0:T(8,128)(2,1)}) custom-call(s32[5]{0:T(128)} %stack.19.refs_0_, s32[8]{0:T(128)} %get-tuple-element.74.refs_1_, bf16[512,128]{1,0:T(8,128)(2,1)} %get-tuple-element.97.refs_2_, ...), custom_call_target="tpu_custom_call" | custom-call | tf_op jit(solution)/shard_map/combine_parts/pallas_call | solution.py:199
  229.6 1.3 collective-permute-done.26.refs_5_
  231.0 2.8 %combine_parts.3 = (bf16[512,128]{1,0:T(8,128)(2,1)}, bf16[512,128]{1,0:T(8,128)(2,1)}, bf16[512,128]{1,0:T(8,128)(2,1)}, bf16[512,128]{1,0:T(8,128)(2,1)}) custom-call(s32[5]{0:T(128)} %stack.19.refs_0_, s32[8]{0:T(128)} %get-tuple-element.74.refs_1_, bf16[512,128]{1,0:T(8,128)(2,1)} %get-tuple-element.84.refs_2_, ...), custom_call_target="tpu_custom_call" | custom-call | tf_op jit(solution)/shard_map/combine_parts/pallas_call | solution.py:199
  234.0 7.2 %collective-permute-start.45 = (bf16[512,128]{1,0:T(8,128)(2,1)}, bf16[512,128]{1,0:T(8,128)(2,1)}, u32[]{:S(2)}, u32[]{:S(2)}) collective-permute-start(bf16[512,128]{1,0:T(8,128)(2,1)} %get-tuple-element.103), channel_id=1, source_target_pairs={{0,16},{1,17},{2,18},{3,19},{4,20},{5,21},{6,22},{7,23},{8,24},{9,... | collective-permute-start | bytes 393224 | tf_op jit(solution)/shard_map/ppermute | solution.py:474
  241.2 0.7 collective-permute-done.35.refs_2_
  241.9 8.6 %collective-permute-start.46 = (bf16[512,128]{1,0:T(8,128)(2,1)}, bf16[512,128]{1,0:T(8,128)(2,1)}, u32[]{:S(2)}, u32[]{:S(2)}) collective-permute-start(bf16[512,128]{1,0:T(8,128)(2,1)} %get-tuple-element.104), channel_id=1, source_target_pairs={{0,24},{1,25},{2,26},{3,27},{4,28},{5,29},{6,30},{7,31},{8,0},{9,1... | collective-permute-start | bytes 393224 | tf_op jit(solution)/shard_map/ppermute | solution.py:474
  250.5 4.1 %collective-permute-start.32 = (bf16[512,128]{1,0:T(8,128)(2,1)}, bf16[512,128]{1,0:T(8,128)(2,1)}, u32[]{:S(2)}, u32[]{:S(2)}) collective-permute-start(bf16[512,128]{1,0:T(8,128)(2,1)} %get-tuple-element.90), channel_id=1, source_target_pairs={{0,16},{1,17},{2,18},{3,19},{4,20},{5,21},{6,22},{7,23},{8,24},{9,... | collective-permute-start | bytes 393224 | tf_op jit(solution)/shard_map/ppermute | solution.py:474
  254.6 3.4 %collective-permute-start.33 = (bf16[512,128]{1,0:T(8,128)(2,1)}, bf16[512,128]{1,0:T(8,128)(2,1)}, u32[]{:S(2)}, u32[]{:S(2)}) collective-permute-start(bf16[512,128]{1,0:T(8,128)(2,1)} %get-tuple-element.91), channel_id=1, source_target_pairs={{0,24},{1,25},{2,26},{3,27},{4,28},{5,29},{6,30},{7,31},{8,0},{9,1... | collective-permute-start | bytes 393224 | tf_op jit(solution)/shard_map/ppermute | solution.py:474
  258.0 1.3 collective-permute-done.45.refs_6_
  259.3 2.2 total_up.1
  261.5 4.8 %collective-permute-done.32.refs_2_ = bf16[512,128]{1,0:T(8,128)(2,1)} collective-permute-done((bf16[512,128]{1,0:T(8,128)(2,1)}, bf16[512,128]{1,0:T(8,128)(2,1)}, u32[]{:S(2)}, u32[]{:S(2)}) %collective-permute-start.32) | collective-permute-done | bytes 131104 | tf_op jit(solution)/shard_map/ppermute | solution.py:474
  266.3 1.8 total_last.1
  (52 shorter events, 2.8 us)
Async XLA Ops:
  2.5 17.8 %collective-permute-start.23 = (bf16[512,128]{1,0:T(8,128)(2,1)}, bf16[512,128]{1,0:T(8,128)(2,1)}, u32[]{:S(2)}, u32[]{:S(2)}) collective-permute-start(bf16[512,128]{1,0:T(8,128)(2,1)} %get-tuple-element.107.refs_2_), channel_id=1, source_target_pairs={{0,24},{1,25},{2,26},{3,27},{4,28},{5,29},{6,30},{7,31},{8,0},{9,1... | collective-permute-start | bytes 393224 | tf_op jit(solution)/shard_map/ppermute | solution.py:458
  7.6 12.8 %collective-permute-start.22 = (bf16[512,128]{1,0:T(8,128)(2,1)}, bf16[512,128]{1,0:T(8,128)(2,1)}, u32[]{:S(2)}, u32[]{:S(2)}) collective-permute-start(bf16[512,128]{1,0:T(8,128)(2,1)} %get-tuple-element.107.refs_2_), channel_id=1, source_target_pairs={{0,16},{1,17},{2,18},{3,19},{4,20},{5,21},{6,22},{7,23},{8,24},{9,... | collective-permute-start | bytes 393224 | tf_op jit(solution)/shard_map/ppermute | solution.py:458
  7.6 12.8 %collective-permute-start.21 = (bf16[512,128]{1,0:T(8,128)(2,1)}, bf16[512,128]{1,0:T(8,128)(2,1)}, u32[]{:S(2)}, u32[]{:S(2)}) collective-permute-start(bf16[512,128]{1,0:T(8,128)(2,1)} %get-tuple-element.107.refs_2_), channel_id=1, source_target_pairs={{0,8},{1,9},{2,10},{3,11},{4,12},{5,13},{6,14},{7,15},{8,16},{9,17... | collective-permute-start | bytes 393224 | tf_op jit(solution)/shard_map/ppermute | solution.py:458
  14.4 0.6 copy-start
  15.0 3.7 %collective-permute-start = (s32[4,9]{1,0:T(4,128)S(1)}, s32[4,9]{1,0:T(4,128)}, u32[]{:S(2)}, u32[]{:S(2)}) collective-permute-start(s32[4,9]{1,0:T(4,128)S(1)} %bitcast.5), channel_id=1, source_target_pairs={{0,4},{1,5},{2,6},{3,7},{4,0},{5,1},{6,2},{7,3},{8,12},{9,13},{10,... | collective-permute-start | bytes 440 | tf_op jit(solution)/shard_map/ppermute | solution.py:484
  23.2 40.6 %all-to-all-start = ((bf16[8,512,128]{2,1,0:T(8,128)(2,1)}), bf16[8,512,128]{2,1,0:T(8,128)(2,1)}, u32[]{:S(2)}, u32[]{:S(2)}) async-start(bf16[8,512,128]{2,1,0:T(8,128)(2,1)} %select_units.5), calls=%async_computation | async-start | bytes 2097152 | tf_op jit(solution)/shard_map/all_to_all | solution.py:469
  27.5 7.2 %collective-permute-start.13 = (bf16[512,128]{1,0:T(8,128)(2,1)}, bf16[512,128]{1,0:T(8,128)(2,1)}, u32[]{:S(2)}, u32[]{:S(2)}) collective-permute-start(bf16[512,128]{1,0:T(8,128)(2,1)} %get-tuple-element.112.refs_2_), channel_id=1, source_target_pairs={{0,24},{1,25},{2,26},{3,27},{4,28},{5,29},{6,30},{7,31},{8,0},{9,1... | collective-permute-start | bytes 393224 | tf_op jit(solution)/shard_map/ppermute | solution.py:458
  30.4 13.6 %collective-permute-start.12 = (bf16[512,128]{1,0:T(8,128)(2,1)}, bf16[512,128]{1,0:T(8,128)(2,1)}, u32[]{:S(2)}, u32[]{:S(2)}) collective-permute-start(bf16[512,128]{1,0:T(8,128)(2,1)} %get-tuple-element.112.refs_2_), channel_id=1, source_target_pairs={{0,16},{1,17},{2,18},{3,19},{4,20},{5,21},{6,22},{7,23},{8,24},{9,... | collective-permute-start | bytes 393224 | tf_op jit(solution)/shard_map/ppermute | solution.py:458
  31.5 12.4 %collective-permute-start.11 = (bf16[512,128]{1,0:T(8,128)(2,1)}, bf16[512,128]{1,0:T(8,128)(2,1)}, u32[]{:S(2)}, u32[]{:S(2)}) collective-permute-start(bf16[512,128]{1,0:T(8,128)(2,1)} %get-tuple-element.112.refs_2_), channel_id=1, source_target_pairs={{0,8},{1,9},{2,10},{3,11},{4,12},{5,13},{6,14},{7,15},{8,16},{9,17... | collective-permute-start | bytes 393224 | tf_op jit(solution)/shard_map/ppermute | solution.py:458
  46.7 5.5 %collective-permute-start.14 = (bf16[512,128]{1,0:T(8,128)(2,1)}, bf16[512,128]{1,0:T(8,128)(2,1)}, u32[]{:S(2)}, u32[]{:S(2)}) collective-permute-start(bf16[512,128]{1,0:T(8,128)(2,1)} %get-tuple-element.65), channel_id=1, source_target_pairs={{0,1},{1,2},{2,3},{3,0},{4,5},{5,6},{6,7},{7,4},{8,9},{9,10},{10,1... | collective-permute-start | bytes 393224 | tf_op jit(solution)/shard_map/ppermute | solution.py:462
  46.8 8.0 %collective-permute-start.15 = (bf16[512,128]{1,0:T(8,128)(2,1)}, bf16[512,128]{1,0:T(8,128)(2,1)}, u32[]{:S(2)}, u32[]{:S(2)}) collective-permute-start(bf16[512,128]{1,0:T(8,128)(2,1)} %get-tuple-element.66), channel_id=1, source_target_pairs={{0,2},{1,3},{2,0},{3,1},{4,6},{5,7},{6,4},{7,5},{8,10},{9,11},{10,... | collective-permute-start | bytes 393224 | tf_op jit(solution)/shard_map/ppermute | solution.py:462
  48.5 10.5 %collective-permute-start.16 = (bf16[512,128]{1,0:T(8,128)(2,1)}, bf16[512,128]{1,0:T(8,128)(2,1)}, u32[]{:S(2)}, u32[]{:S(2)}) collective-permute-start(bf16[512,128]{1,0:T(8,128)(2,1)} %get-tuple-element.67), channel_id=1, source_target_pairs={{0,3},{1,0},{2,1},{3,2},{4,7},{5,4},{6,5},{7,6},{8,11},{9,8},{10,9... | collective-permute-start | bytes 393224 | tf_op jit(solution)/shard_map/ppermute | solution.py:462
  49.9 9.2 %collective-permute-start.17 = (bf16[512,128]{1,0:T(8,128)(2,1)}, bf16[512,128]{1,0:T(8,128)(2,1)}, u32[]{:S(2)}, u32[]{:S(2)}) collective-permute-start(bf16[512,128]{1,0:T(8,128)(2,1)} %get-tuple-element.68), channel_id=1, source_target_pairs={{0,4},{1,5},{2,6},{3,7},{4,0},{5,1},{6,2},{7,3},{8,12},{9,13},{10,... | collective-permute-start | bytes 393224 | tf_op jit(solution)/shard_map/ppermute | solution.py:462
  51.4 10.6 %collective-permute-start.18 = (bf16[512,128]{1,0:T(8,128)(2,1)}, bf16[512,128]{1,0:T(8,128)(2,1)}, u32[]{:S(2)}, u32[]{:S(2)}) collective-permute-start(bf16[512,128]{1,0:T(8,128)(2,1)} %get-tuple-element.69), channel_id=1, source_target_pairs={{0,5},{1,6},{2,7},{3,4},{4,1},{5,2},{6,3},{7,0},{8,13},{9,14},{10,... | collective-permute-start | bytes 393224 | tf_op jit(solution)/shard_map/ppermute | solution.py:462
  52.2 10.1 %collective-permute-start.19 = (bf16[512,128]{1,0:T(8,128)(2,1)}, bf16[512,128]{1,0:T(8,128)(2,1)}, u32[]{:S(2)}, u32[]{:S(2)}) collective-permute-start(bf16[512,128]{1,0:T(8,128)(2,1)} %get-tuple-element.70), channel_id=1, source_target_pairs={{0,6},{1,7},{2,4},{3,5},{4,2},{5,3},{6,0},{7,1},{8,14},{9,15},{10,... | collective-permute-start | bytes 393224 | tf_op jit(solution)/shard_map/ppermute | solution.py:462
  54.8 9.0 %collective-permute-start.20 = (bf16[512,128]{1,0:T(8,128)(2,1)}, bf16[512,128]{1,0:T(8,128)(2,1)}, u32[]{:S(2)}, u32[]{:S(2)}) collective-permute-start(bf16[512,128]{1,0:T(8,128)(2,1)} %get-tuple-element.71), channel_id=1, source_target_pairs={{0,7},{1,4},{2,5},{3,6},{4,3},{5,0},{6,1},{7,2},{8,15},{9,12},{10,... | collective-permute-start | bytes 393224 | tf_op jit(solution)/shard_map/ppermute | solution.py:462
  59.0 48.8 %collective-permute-start.3 = (bf16[512,256]{1,0:T(8,128)(2,1)}, bf16[512,256]{1,0:T(8,128)(2,1)}, u32[]{:S(2)}, u32[]{:S(2)}) collective-permute-start(bf16[512,256]{1,0:T(8,128)(2,1)} %pad_maximum_fusion.refs_2_), channel_id=1, source_target_pairs={{0,24},{1,25},{2,26},{3,27},{4,28},{5,29},{6,30},{7,31},{8,0},{9,1... | collective-permute-start | bytes 786440 | tf_op jit(solution)/shard_map/ppermute | solution.py:458
  59.1 48.8 %collective-permute-start.2 = (bf16[512,256]{1,0:T(8,128)(2,1)}, bf16[512,256]{1,0:T(8,128)(2,1)}, u32[]{:S(2)}, u32[]{:S(2)}) collective-permute-start(bf16[512,256]{1,0:T(8,128)(2,1)} %pad_maximum_fusion.refs_2_), channel_id=1, source_target_pairs={{0,16},{1,17},{2,18},{3,19},{4,20},{5,21},{6,22},{7,23},{8,24},{9,... | collective-permute-start | bytes 786440 | tf_op jit(solution)/shard_map/ppermute | solution.py:458
  62.0 45.9 %collective-permute-start.1 = (bf16[512,256]{1,0:T(8,128)(2,1)}, bf16[512,256]{1,0:T(8,128)(2,1)}, u32[]{:S(2)}, u32[]{:S(2)}) collective-permute-start(bf16[512,256]{1,0:T(8,128)(2,1)} %pad_maximum_fusion.refs_2_), channel_id=1, source_target_pairs={{0,8},{1,9},{2,10},{3,11},{4,12},{5,13},{6,14},{7,15},{8,16},{9,17... | collective-permute-start | bytes 786440 | tf_op jit(solution)/shard_map/ppermute | solution.py:458
  103.3 95.2 %all-to-all-start.1 = ((bf16[8,512,256]{2,1,0:T(8,128)(2,1)}), bf16[8,512,256]{2,1,0:T(8,128)(2,1)}, u32[]{:S(2)}, u32[]{:S(2)}) async-start(bf16[8,512,256]{2,1,0:T(8,128)(2,1)} %get-tuple-element.75), calls=%async_computation.1 | async-start | bytes 4194304 | tf_op jit(solution)/shard_map/all_to_all | solution.py:469
  111.2 26.7 %collective-permute-start.4 = (bf16[512,256]{1,0:T(8,128)(2,1)}, bf16[512,256]{1,0:T(8,128)(2,1)}, u32[]{:S(2)}, u32[]{:S(2)}) collective-permute-start(bf16[512,256]{1,0:T(8,128)(2,1)} %get-tuple-element.57), channel_id=1, source_target_pairs={{0,1},{1,2},{2,3},{3,0},{4,5},{5,6},{6,7},{7,4},{8,9},{9,10},{10,1... | collective-permute-start | bytes 786440 | tf_op jit(solution)/shard_map/ppermute | solution.py:462
  111.9 28.8 %collective-permute-start.5 = (bf16[512,256]{1,0:T(8,128)(2,1)}, bf16[512,256]{1,0:T(8,128)(2,1)}, u32[]{:S(2)}, u32[]{:S(2)}) collective-permute-start(bf16[512,256]{1,0:T(8,128)(2,1)} %get-tuple-element.58), channel_id=1, source_target_pairs={{0,2},{1,3},{2,0},{3,1},{4,6},{5,7},{6,4},{7,5},{8,10},{9,11},{10,... | collective-permute-start | bytes 786440 | tf_op jit(solution)/shard_map/ppermute | solution.py:462
  114.5 30.8 %collective-permute-start.6 = (bf16[512,256]{1,0:T(8,128)(2,1)}, bf16[512,256]{1,0:T(8,128)(2,1)}, u32[]{:S(2)}, u32[]{:S(2)}) collective-permute-start(bf16[512,256]{1,0:T(8,128)(2,1)} %get-tuple-element.59), channel_id=1, source_target_pairs={{0,3},{1,0},{2,1},{3,2},{4,7},{5,4},{6,5},{7,6},{8,11},{9,8},{10,9... | collective-permute-start | bytes 786440 | tf_op jit(solution)/shard_map/ppermute | solution.py:462
  115.9 29.4 %collective-permute-start.7 = (bf16[512,256]{1,0:T(8,128)(2,1)}, bf16[512,256]{1,0:T(8,128)(2,1)}, u32[]{:S(2)}, u32[]{:S(2)}) collective-permute-start(bf16[512,256]{1,0:T(8,128)(2,1)} %get-tuple-element.60), channel_id=1, source_target_pairs={{0,4},{1,5},{2,6},{3,7},{4,0},{5,1},{6,2},{7,3},{8,12},{9,13},{10,... | collective-permute-start | bytes 786440 | tf_op jit(solution)/shard_map/ppermute | solution.py:462
  116.5 34.5 %collective-permute-start.8 = (bf16[512,256]{1,0:T(8,128)(2,1)}, bf16[512,256]{1,0:T(8,128)(2,1)}, u32[]{:S(2)}, u32[]{:S(2)}) collective-permute-start(bf16[512,256]{1,0:T(8,128)(2,1)} %get-tuple-element.61), channel_id=1, source_target_pairs={{0,5},{1,6},{2,7},{3,4},{4,1},{5,2},{6,3},{7,0},{8,13},{9,14},{10,... | collective-permute-start | bytes 786440 | tf_op jit(solution)/shard_map/ppermute | solution.py:462
  137.9 14.3 %collective-permute-start.9 = (bf16[512,256]{1,0:T(8,128)(2,1)}, bf16[512,256]{1,0:T(8,128)(2,1)}, u32[]{:S(2)}, u32[]{:S(2)}) collective-permute-start(bf16[512,256]{1,0:T(8,128)(2,1)} %get-tuple-element.62), channel_id=1, source_target_pairs={{0,6},{1,7},{2,4},{3,5},{4,2},{5,3},{6,0},{7,1},{8,14},{9,15},{10,... | collective-permute-start | bytes 786440 | tf_op jit(solution)/shard_map/ppermute | solution.py:462
  140.8 19.1 %collective-permute-start.10 = (bf16[512,256]{1,0:T(8,128)(2,1)}, bf16[512,256]{1,0:T(8,128)(2,1)}, u32[]{:S(2)}, u32[]{:S(2)}) collective-permute-start(bf16[512,256]{1,0:T(8,128)(2,1)} %get-tuple-element.63), channel_id=1, source_target_pairs={{0,7},{1,4},{2,5},{3,6},{4,3},{5,0},{6,1},{7,2},{8,15},{9,12},{10,... | collective-permute-start | bytes 786440 | tf_op jit(solution)/shard_map/ppermute | solution.py:462
  198.5 6.8 %collective-permute-start.27 = (bf16[512,128]{1,0:T(8,128)(2,1)}, bf16[512,128]{1,0:T(8,128)(2,1)}, u32[]{:S(2)}, u32[]{:S(2)}) collective-permute-start(bf16[512,128]{1,0:T(8,128)(2,1)} %get-tuple-element.84.refs_2_), channel_id=1, source_target_pairs={{0,4},{1,5},{2,6},{3,7},{4,0},{5,1},{6,2},{7,3},{8,12},{9,13},{10,... | collective-permute-start | bytes 393224 | tf_op jit(solution)/shard_map/ppermute | solution.py:462
  198.6 7.4 %collective-permute-start.28 = (bf16[512,128]{1,0:T(8,128)(2,1)}, bf16[512,128]{1,0:T(8,128)(2,1)}, u32[]{:S(2)}, u32[]{:S(2)}) collective-permute-start(bf16[512,128]{1,0:T(8,128)(2,1)} %get-tuple-element.85), channel_id=1, source_target_pairs={{0,5},{1,6},{2,7},{3,4},{4,1},{5,2},{6,3},{7,0},{8,13},{9,14},{10,... | collective-permute-start | bytes 393224 | tf_op jit(solution)/shard_map/ppermute | solution.py:462
  198.6 7.6 %collective-permute-start.24 = (bf16[512,128]{1,0:T(8,128)(2,1)}, bf16[512,128]{1,0:T(8,128)(2,1)}, u32[]{:S(2)}, u32[]{:S(2)}) collective-permute-start(bf16[512,128]{1,0:T(8,128)(2,1)} %get-tuple-element.85), channel_id=1, source_target_pairs={{0,1},{1,2},{2,3},{3,0},{4,5},{5,6},{6,7},{7,4},{8,9},{9,10},{10,1... | collective-permute-start | bytes 393224 | tf_op jit(solution)/shard_map/ppermute | solution.py:462
  202.4 9.8 %collective-permute-start.29 = (bf16[512,128]{1,0:T(8,128)(2,1)}, bf16[512,128]{1,0:T(8,128)(2,1)}, u32[]{:S(2)}, u32[]{:S(2)}) collective-permute-start(bf16[512,128]{1,0:T(8,128)(2,1)} %get-tuple-element.86), channel_id=1, source_target_pairs={{0,6},{1,7},{2,4},{3,5},{4,2},{5,3},{6,0},{7,1},{8,14},{9,15},{10,... | collective-permute-start | bytes 393224 | tf_op jit(solution)/shard_map/ppermute | solution.py:462
  202.4 11.7 %collective-permute-start.25 = (bf16[512,128]{1,0:T(8,128)(2,1)}, bf16[512,128]{1,0:T(8,128)(2,1)}, u32[]{:S(2)}, u32[]{:S(2)}) collective-permute-start(bf16[512,128]{1,0:T(8,128)(2,1)} %get-tuple-element.86), channel_id=1, source_target_pairs={{0,2},{1,3},{2,0},{3,1},{4,6},{5,7},{6,4},{7,5},{8,10},{9,11},{10,... | collective-permute-start | bytes 393224 | tf_op jit(solution)/shard_map/ppermute | solution.py:462
  205.2 8.9 %collective-permute-start.40 = (bf16[512,128]{1,0:T(8,128)(2,1)}, bf16[512,128]{1,0:T(8,128)(2,1)}, u32[]{:S(2)}, u32[]{:S(2)}) collective-permute-start(bf16[512,128]{1,0:T(8,128)(2,1)} %get-tuple-element.97.refs_2_), channel_id=1, source_target_pairs={{0,4},{1,5},{2,6},{3,7},{4,0},{5,1},{6,2},{7,3},{8,12},{9,13},{10,... | collective-permute-start | bytes 393224 | tf_op jit(solution)/shard_map/ppermute | solution.py:462
  205.9 12.8 %collective-permute-start.41 = (bf16[512,128]{1,0:T(8,128)(2,1)}, bf16[512,128]{1,0:T(8,128)(2,1)}, u32[]{:S(2)}, u32[]{:S(2)}) collective-permute-start(bf16[512,128]{1,0:T(8,128)(2,1)} %get-tuple-element.98), channel_id=1, source_target_pairs={{0,5},{1,6},{2,7},{3,4},{4,1},{5,2},{6,3},{7,0},{8,13},{9,14},{10,... | collective-permute-start | bytes 393224 | tf_op jit(solution)/shard_map/ppermute | solution.py:462
  206.2 13.1 %collective-permute-start.37 = (bf16[512,128]{1,0:T(8,128)(2,1)}, bf16[512,128]{1,0:T(8,128)(2,1)}, u32[]{:S(2)}, u32[]{:S(2)}) collective-permute-start(bf16[512,128]{1,0:T(8,128)(2,1)} %get-tuple-element.98), channel_id=1, source_target_pairs={{0,1},{1,2},{2,3},{3,0},{4,5},{5,6},{6,7},{7,4},{8,9},{9,10},{10,1... | collective-permute-start | bytes 393224 | tf_op jit(solution)/shard_map/ppermute | solution.py:462
  212.3 7.6 %collective-permute-start.42 = (bf16[512,128]{1,0:T(8,128)(2,1)}, bf16[512,128]{1,0:T(8,128)(2,1)}, u32[]{:S(2)}, u32[]{:S(2)}) collective-permute-start(bf16[512,128]{1,0:T(8,128)(2,1)} %get-tuple-element.99), channel_id=1, source_target_pairs={{0,6},{1,7},{2,4},{3,5},{4,2},{5,3},{6,0},{7,1},{8,14},{9,15},{10,... | collective-permute-start | bytes 393224 | tf_op jit(solution)/shard_map/ppermute | solution.py:462
  214.1 7.7 %collective-permute-start.38 = (bf16[512,128]{1,0:T(8,128)(2,1)}, bf16[512,128]{1,0:T(8,128)(2,1)}, u32[]{:S(2)}, u32[]{:S(2)}) collective-permute-start(bf16[512,128]{1,0:T(8,128)(2,1)} %get-tuple-element.99), channel_id=1, source_target_pairs={{0,2},{1,3},{2,0},{3,1},{4,6},{5,7},{6,4},{7,5},{8,10},{9,11},{10,... | collective-permute-start | bytes 393224 | tf_op jit(solution)/shard_map/ppermute | solution.py:462
  214.1 9.2 %collective-permute-start.43 = (bf16[512,128]{1,0:T(8,128)(2,1)}, bf16[512,128]{1,0:T(8,128)(2,1)}, u32[]{:S(2)}, u32[]{:S(2)}) collective-permute-start(bf16[512,128]{1,0:T(8,128)(2,1)} %get-tuple-element.100), channel_id=1, source_target_pairs={{0,7},{1,4},{2,5},{3,6},{4,3},{5,0},{6,1},{7,2},{8,15},{9,12},{10,... | collective-permute-start | bytes 393224 | tf_op jit(solution)/shard_map/ppermute | solution.py:462
  218.8 8.0 %collective-permute-start.39 = (bf16[512,128]{1,0:T(8,128)(2,1)}, bf16[512,128]{1,0:T(8,128)(2,1)}, u32[]{:S(2)}, u32[]{:S(2)}) collective-permute-start(bf16[512,128]{1,0:T(8,128)(2,1)} %get-tuple-element.100), channel_id=1, source_target_pairs={{0,3},{1,0},{2,1},{3,2},{4,7},{5,4},{6,5},{7,6},{8,11},{9,8},{10,9... | collective-permute-start | bytes 393224 | tf_op jit(solution)/shard_map/ppermute | solution.py:462
  219.3 14.7 %collective-permute-start.34 = (bf16[512,256]{1,0:T(8,128)(2,1)}, bf16[512,256]{1,0:T(8,128)(2,1)}, u32[]{:S(2)}, u32[]{:S(2)}) collective-permute-start(bf16[512,256]{1,0:T(8,128)(2,1)} %get-tuple-element.94), channel_id=1, source_target_pairs={{0,8},{1,9},{2,10},{3,11},{4,12},{5,13},{6,14},{7,15},{8,16},{9,17... | collective-permute-start | bytes 786440 | tf_op jit(solution)/shard_map/ppermute | solution.py:474
  219.9 22.1 %collective-permute-start.35 = (bf16[512,256]{1,0:T(8,128)(2,1)}, bf16[512,256]{1,0:T(8,128)(2,1)}, u32[]{:S(2)}, u32[]{:S(2)}) collective-permute-start(bf16[512,256]{1,0:T(8,128)(2,1)} %get-tuple-element.95), channel_id=1, source_target_pairs={{0,16},{1,17},{2,18},{3,19},{4,20},{5,21},{6,22},{7,23},{8,24},{9,... | collective-permute-start | bytes 786440 | tf_op jit(solution)/shard_map/ppermute | solution.py:474
  221.9 28.7 %collective-permute-start.36 = (bf16[512,256]{1,0:T(8,128)(2,1)}, bf16[512,256]{1,0:T(8,128)(2,1)}, u32[]{:S(2)}, u32[]{:S(2)}) collective-permute-start(bf16[512,256]{1,0:T(8,128)(2,1)} %get-tuple-element.96), channel_id=1, source_target_pairs={{0,24},{1,25},{2,26},{3,27},{4,28},{5,29},{6,30},{7,31},{8,0},{9,1... | collective-permute-start | bytes 786440 | tf_op jit(solution)/shard_map/ppermute | solution.py:474
  223.4 6.2 %collective-permute-start.30 = (bf16[512,128]{1,0:T(8,128)(2,1)}, bf16[512,128]{1,0:T(8,128)(2,1)}, u32[]{:S(2)}, u32[]{:S(2)}) collective-permute-start(bf16[512,128]{1,0:T(8,128)(2,1)} %get-tuple-element.87), channel_id=1, source_target_pairs={{0,7},{1,4},{2,5},{3,6},{4,3},{5,0},{6,1},{7,2},{8,15},{9,12},{10,... | collective-permute-start | bytes 393224 | tf_op jit(solution)/shard_map/ppermute | solution.py:462
  226.8 4.2 %collective-permute-start.26 = (bf16[512,128]{1,0:T(8,128)(2,1)}, bf16[512,128]{1,0:T(8,128)(2,1)}, u32[]{:S(2)}, u32[]{:S(2)}) collective-permute-start(bf16[512,128]{1,0:T(8,128)(2,1)} %get-tuple-element.87), channel_id=1, source_target_pairs={{0,3},{1,0},{2,1},{3,2},{4,7},{5,4},{6,5},{7,6},{8,11},{9,8},{10,9... | collective-permute-start | bytes 393224 | tf_op jit(solution)/shard_map/ppermute | solution.py:462
  229.6 25.0 %collective-permute-start.44 = (bf16[512,128]{1,0:T(8,128)(2,1)}, bf16[512,128]{1,0:T(8,128)(2,1)}, u32[]{:S(2)}, u32[]{:S(2)}) collective-permute-start(bf16[512,128]{1,0:T(8,128)(2,1)} %get-tuple-element.102), channel_id=1, source_target_pairs={{0,8},{1,9},{2,10},{3,11},{4,12},{5,13},{6,14},{7,15},{8,16},{9,17... | collective-permute-start | bytes 393224 | tf_op jit(solution)/shard_map/ppermute | solution.py:474
  233.8 27.8 %collective-permute-start.31 = (bf16[512,128]{1,0:T(8,128)(2,1)}, bf16[512,128]{1,0:T(8,128)(2,1)}, u32[]{:S(2)}, u32[]{:S(2)}) collective-permute-start(bf16[512,128]{1,0:T(8,128)(2,1)} %get-tuple-element.89), channel_id=1, source_target_pairs={{0,8},{1,9},{2,10},{3,11},{4,12},{5,13},{6,14},{7,15},{8,16},{9,17... | collective-permute-start | bytes 393224 | tf_op jit(solution)/shard_map/ppermute | solution.py:474
  234.0 25.3 %collective-permute-start.45 = (bf16[512,128]{1,0:T(8,128)(2,1)}, bf16[512,128]{1,0:T(8,128)(2,1)}, u32[]{:S(2)}, u32[]{:S(2)}) collective-permute-start(bf16[512,128]{1,0:T(8,128)(2,1)} %get-tuple-element.103), channel_id=1, source_target_pairs={{0,16},{1,17},{2,18},{3,19},{4,20},{5,21},{6,22},{7,23},{8,24},{9,... | collective-permute-start | bytes 393224 | tf_op jit(solution)/shard_map/ppermute | solution.py:474
  241.9 17.4 %collective-permute-start.46 = (bf16[512,128]{1,0:T(8,128)(2,1)}, bf16[512,128]{1,0:T(8,128)(2,1)}, u32[]{:S(2)}, u32[]{:S(2)}) collective-permute-start(bf16[512,128]{1,0:T(8,128)(2,1)} %get-tuple-element.104), channel_id=1, source_target_pairs={{0,24},{1,25},{2,26},{3,27},{4,28},{5,29},{6,30},{7,31},{8,0},{9,1... | collective-permute-start | bytes 393224 | tf_op jit(solution)/shard_map/ppermute | solution.py:474
  250.5 15.8 %collective-permute-start.32 = (bf16[512,128]{1,0:T(8,128)(2,1)}, bf16[512,128]{1,0:T(8,128)(2,1)}, u32[]{:S(2)}, u32[]{:S(2)}) collective-permute-start(bf16[512,128]{1,0:T(8,128)(2,1)} %get-tuple-element.90), channel_id=1, source_target_pairs={{0,16},{1,17},{2,18},{3,19},{4,20},{5,21},{6,22},{7,23},{8,24},{9,... | collective-permute-start | bytes 393224 | tf_op jit(solution)/shard_map/ppermute | solution.py:474
  254.6 11.7 %collective-permute-start.33 = (bf16[512,128]{1,0:T(8,128)(2,1)}, bf16[512,128]{1,0:T(8,128)(2,1)}, u32[]{:S(2)}, u32[]{:S(2)}) collective-permute-start(bf16[512,128]{1,0:T(8,128)(2,1)} %get-tuple-element.91), channel_id=1, source_target_pairs={{0,24},{1,25},{2,26},{3,27},{4,28},{5,29},{6,30},{7,31},{8,0},{9,1... | collective-permute-start | bytes 393224 | tf_op jit(solution)/shard_map/ppermute | solution.py:474
